TPU v7x, 512 devices: a whole 4x8x8 slice. The times are simulated.
512 devices in a mesh: dp: 8 (over z_hi, core), seq: 64 (over z_lo, y, x).
Axes of the slice: x: 4, y: 8, z: 8 (z_hi: 4, z_lo: 2; z = z_hi * 2 + z_lo), core: 2. Of those that a mesh axis runs over, the one named last changes fastest.
Arguments:
- qkv: bfloat16 [8, 64, 128, 1728], P('dp', 'seq'), may hold values from -7 to 7
- segment_ids: int32 [8, 64], P('dp'), may hold values from 0 to 3, never falling along the last dimension, each value on 1 to 32 neighbouring positions
- upstream: bfloat16 [8, 64, 128, 1152], P('dp', 'seq'), may hold values from -6 to 6
- out_weight: bfloat16 [576, 1152], P('dp'), may hold values from -0.25 to 0.25
Outputs:
- output: bfloat16 [8, 64, 128, 1152], P('dp', 'seq')
- qkv_grad: bfloat16 [8, 64, 128, 1728], P('dp', 'seq')
- weight_grad: float32 [576, 1152], P('dp')
Inputs may be any that keep to these rules, and one draw needn't show every extreme that they name: `segment_ids`: within a clip the id never falls from one frame to the next; a segment covers at most 32 frames and one segment of every clip covers exactly that many.
All inputs are finite; a program needn't handle non-finite values.
Results may differ from a plain program's by a relative error of at most 0.006.
Values may be sent and summed in bfloat16 or wider, within the bound.
A program may use at most 64 MiB of HBM per device.

v0:
```python
import math

import jax
import jax.numpy as jnp
from jax import lax
from jax.sharding import PartitionSpec as P

HEAD_DIM = 72
HEADS = 8


def forward_attend(stacked, allowed, factor):
    clip_count, frame_count, pos_here, packed = stacked.shape
    head_split = stacked.reshape(clip_count, frame_count, pos_here, 3, HEADS, HEAD_DIM)
    queries = head_split[:, :, :, 0]
    key_part = head_split[:, :, :, 1]
    value_part = head_split[:, :, :, 2]
    scores = (
        jnp.einsum("cfphd,cgphd->cphfg", queries, key_part, preferred_element_type=jnp.float32)
        * factor
    )
    scores = jnp.where(allowed, scores, jnp.float32(-1e30))
    row_peak = jnp.max(scores, axis=-1, keepdims=True)
    exponent = jnp.exp(scores - row_peak)
    attend = exponent / jnp.sum(exponent, axis=-1, keepdims=True)
    attend_low = attend.astype(jnp.bfloat16)
    mixed_pos = jnp.einsum(
        "cphfg,cgphd->cfphd", attend_low, value_part, preferred_element_type=jnp.float32
    )
    mixed_pos = mixed_pos.astype(jnp.bfloat16).reshape(
        clip_count, frame_count, pos_here, HEADS * HEAD_DIM
    )
    return (mixed_pos, attend, attend_low, queries, key_part, value_part)


def backward_attend(saved, grad_pos_in, factor):
    attend, attend_low, queries, key_part, value_part = saved
    clip_count, frame_count, pos_here = grad_pos_in.shape[:3]
    grad_heads = grad_pos_in.reshape(clip_count, frame_count, pos_here, HEADS, HEAD_DIM)
    attend_grad = jnp.einsum(
        "cfphd,cgphd->cphfg", grad_heads, value_part, preferred_element_type=jnp.float32
    )
    row_dot = jnp.sum(attend * attend_grad, axis=-1, keepdims=True)
    score_grad = (attend * (attend_grad - row_dot)).astype(jnp.bfloat16)
    query_grad = (
        jnp.einsum("cphfg,cgphd->cfphd", score_grad, key_part, preferred_element_type=jnp.float32)
        * factor
    ).astype(jnp.bfloat16)
    key_grad = (
        jnp.einsum("cphfg,cfphd->cgphd", score_grad, queries, preferred_element_type=jnp.float32)
        * factor
    ).astype(jnp.bfloat16)
    value_grad = jnp.einsum(
        "cphfg,cfphd->cgphd", attend_low, grad_heads, preferred_element_type=jnp.float32
    ).astype(jnp.bfloat16)
    stacked_grad = jnp.stack([query_grad, key_grad, value_grad], axis=3)
    return stacked_grad.reshape(clip_count, frame_count, pos_here, 3 * HEADS * HEAD_DIM)


def on_device(qkv, segment_ids, upstream, out_weight):
    clip_count, frames_here, positions, packed = qkv.shape
    inner_width = HEADS * HEAD_DIM
    factor = 1.0 / math.sqrt(HEAD_DIM)
    full_weight = lax.all_gather(out_weight, "dp", axis=0, tiled=True)
    model_width = full_weight.shape[1]
    upstream_flat = upstream.reshape(-1, model_width)
    allowed = (segment_ids[:, :, None] == segment_ids[:, None, :])[:, None, None, :, :]
    stacked = lax.all_to_all(qkv, "seq", split_axis=2, concat_axis=1, tiled=True)
    mixed_pos, attend, attend_low, queries, key_part, value_part = forward_attend(
        stacked, allowed, factor
    )
    mixed_frames = lax.all_to_all(mixed_pos, "seq", split_axis=1, concat_axis=2, tiled=True)
    product = lax.dot_general(
        upstream_flat, full_weight, (((1,), (1,)), ((), ())), preferred_element_type=jnp.float32
    )
    grad_frames_in = product.astype(jnp.bfloat16).reshape(
        clip_count, frames_here, positions, inner_width
    )
    grad_pos_in = lax.all_to_all(grad_frames_in, "seq", split_axis=2, concat_axis=1, tiled=True)
    grad_pos = backward_attend(
        (attend, attend_low, queries, key_part, value_part), grad_pos_in, factor
    )
    qkv_grad = lax.all_to_all(grad_pos, "seq", split_axis=1, concat_axis=2, tiled=True)
    mixed_flat = mixed_frames.reshape(-1, inner_width)
    output = jnp.dot(mixed_flat, full_weight, preferred_element_type=jnp.float32).astype(
        jnp.bfloat16
    )
    output = output.reshape(clip_count, frames_here, positions, model_width)
    partial_value = lax.dot_general(
        mixed_flat, upstream_flat, (((0,), (0,)), ((), ())), preferred_element_type=jnp.float32
    )
    total_tokens = mixed_flat.shape[0] * lax.axis_size("dp") * lax.axis_size("seq")
    summed_all = lax.psum(partial_value, "seq")
    weight_share = lax.psum_scatter(summed_all, "dp", scatter_dimension=0, tiled=True)
    weight_grad = weight_share / math.sqrt(total_tokens)
    return (output, qkv_grad, weight_grad)


def solution(mesh):
    in_specs = (
        P("dp", "seq", None, None),
        P("dp", None),
        P("dp", "seq", None, None),
        P("dp", None),
    )
    out_specs = (P("dp", "seq", None, None), P("dp", "seq", None, None), P("dp", None))
    return jax.shard_map(
        on_device, mesh=mesh, in_specs=in_specs, out_specs=out_specs, check_vma=False
    )
```

profile of v0, /device:TPU:64, one launch (start us, length us, event | category | flops | bytes accessed | tf_op | source)
XLA Modules:
  0.0 704.2 jit_solution(5261886630118157462)
XLA Ops:
  7.2 2.4 copy.25
  9.6 0.5 broadcast.61
  10.1 3.5 reduce.10
  13.7 0.9 reshape.174
  14.6 11.7 %all-to-all-start = ((bf16[64,2,1728]{2,1,0:T(2,128)(2,1)}), bf16[64,2,1728]{2,1,0:T(2,128)(2,1)S(1)}, u32[]{:S(2)}, u32[]{:S(2)}) async-start(bf16[64,2,1728]{2,1,0:T(2,128)(2,1)} %reshape.174), calls=%async_computation | async-start | bytes 917504 | tf_op jit(solution)/shard_map/all_to_all | solution.py:68
  26.3 0.0 all-gather.2.cloned.1.call-start
  26.3 0.7 all-gather.2.cloned.1.call-update
  27.0 0.0 reduce-scatter.4.cloned.1.call-start
  27.1 0.1 broadcast_compare_fusion
  27.2 14.2 %all-to-all-done = bf16[64,2,1728]{2,1,0:T(2,128)(2,1)S(1)} async-done(((bf16[64,2,1728]{2,1,0:T(2,128)(2,1)}), bf16[64,2,1728]{2,1,0:T(2,128)(2,1)S(1)}, u32[]{:S(2)}, u32[]{:S(2)}) %all-to-all-start) | async-done | bytes 442400 | tf_op jit(solution)/shard_map/all_to_all | solution.py:68
  41.4 0.4 reshape.175
  41.8 2.6 bitcast_reduce_fusion
  44.4 0.9 reshape.158
  45.2 0.1 fusion.20
  45.4 0.3 fusion.4
  45.7 0.9 fusion.21
  46.6 0.3 fusion.9
  46.9 0.2 copy.41
  47.1 0.5 reshape.169
  47.6 17.0 %all_to_all.19 = bf16[1,64,2,576]{3,2,0,1:T(2,128)(2,1)S(1)} all-to-all(bf16[1,64,2,576]{3,2,0,1:T(2,128)(2,1)S(1)} %reshape.169), channel_id=1, replica_groups=mesh['dp'=8,'seq'=64] {'seq'}, dimensions={1} | all-to-all | bytes 294912 | tf_op jit(solution)/shard_map/all_to_all | solution.py:72
  64.6 0.1 reshape.163
  64.7 2.1 fusion.12
  66.8 0.0 reduce-scatter.4.cloned.1.call-update
  66.8 0.0 all-gather.2.cloned.1.call-done
  66.9 1.8 fusion.11
  68.7 0.2 copy.32
  68.9 1.7 reduce.11
  70.6 0.1 reshape.176
  70.7 22.7 %all_to_all.40 = bf16[64,2,576]{2,1,0:T(2,128)(2,1)S(1)} all-to-all(bf16[64,2,576]{2,1,0:T(2,128)(2,1)S(1)} %reshape.176), channel_id=1, replica_groups=mesh['dp'=8,'seq'=64] {'seq'}, dimensions={0} | all-to-all | bytes 294912 | tf_op jit(solution)/shard_map/all_to_all | solution.py:79
  93.4 0.1 reshape.177
  93.6 0.9 bitcast_reduce_fusion.1
  94.5 0.3 reshape.167
  94.8 0.3 fusion.10
  95.0 0.3 multiply_reduce_fusion
  95.3 0.1 multiply_convert_fusion
  95.4 0.3 fusion.8
  95.7 0.2 fusion.7
  95.9 0.2 pad_maximum_fusion
  96.1 0.5 copy.42
  96.7 2.2 reshape.170
  98.9 5.9 all-to-all-start.3
  104.8 0.0 all-reduce.3.cloned.1.call-start
  104.8 20.2 %reduce-scatter.4.cloned.1.call-done = f32[72,1152]{1,0:T(8,128)} async-done(((f32[576,1152]{1,0:T(8,128)}), f32[72,1152]{1,0:T(8,128)}) %reduce-scatter.4.cloned.1.call-update) | async-done | bytes 331792
  125.0 1.1 fusion.1
  126.2 0.3 all_to_all.14
  126.5 1.0 copy.38
  127.5 568.5 %all-reduce.3.cloned.1.call-done = f32[72,1152]{1,0:T(8,128)} async-done(((f32[72,1152]{1,0:T(8,128)}), f32[72,1152]{1,0:T(8,128)}) %all-reduce.3.cloned.1.call-update) | async-done | bytes 331792 | tf_op jit(solution)/shard_map/psum | solution.py:93
  695.9 1.7 broadcast_multiply_fusion
  (8 shorter events, 0.0 us)
Async XLA Ops:
  7.2 57.6 %copy-start = (bf16[1,1,128,1152]{3,2,1,0:T(8,128)(2,1)S(1)}, bf16[1,1,128,1152]{3,2,1,0:T(8,128)(2,1)}, u32[]{:S(2)}) copy-start(bf16[1,1,128,1152]{3,2,1,0:T(8,128)(2,1)} %param.6) | copy-start | bytes 884740
  13.7 13.4 %copy-start.2 = (s32[1,64]{1,0:T(1,128)S(1)}, s32[1,64]{1,0:T(1,128)}, u32[]{:S(2)}) copy-start(s32[1,64]{1,0:T(1,128)} %param.5) | copy-start | bytes 772
  14.6 26.8 %all-to-all-start = ((bf16[64,2,1728]{2,1,0:T(2,128)(2,1)}), bf16[64,2,1728]{2,1,0:T(2,128)(2,1)S(1)}, u32[]{:S(2)}, u32[]{:S(2)}) async-start(bf16[64,2,1728]{2,1,0:T(2,128)(2,1)} %reshape.174), calls=%async_computation | async-start | bytes 917504 | tf_op jit(solution)/shard_map/all_to_all | solution.py:68
  26.3 40.5 %all-gather.2.cloned.1.call-start = ((), (), s32[]{:S(2)}) async-start(), calls=%async_computation.5 | async-start | bytes 1492992 | tf_op jit(solution)/shard_map/all_gather | solution.py:64
  27.0 98.0 %reduce-scatter.4.cloned.1.call-start = ((), (), s32[]{:S(2)}) async-start(), calls=%async_computation.7 | async-start | bytes 2985984
  96.7 28.4 %copy-start.1 = (bf16[576,1152]{1,0:T(8,128)(2,1)S(1)}, bf16[576,1152]{1,0:T(8,128)(2,1)}, u32[]{:S(2)}) copy-start(bf16[576,1152]{1,0:T(8,128)(2,1)} %all-gather.2.cloned.1.call-done) | copy-start | bytes 3981316
  98.9 27.3 %all-to-all-start.3 = ((bf16[1,64,2,1728]{3,2,0,1:T(2,128)(2,1)}), bf16[1,64,2,1728]{3,2,0,1:T(2,128)(2,1)S(1)}, u32[]{:S(2)}, u32[]{:S(2)}) async-start(bf16[1,64,2,1728]{3,2,0,1:T(2,128)(2,1)} %reshape.170), calls=%async_computation.3 | async-start | bytes 917504 | tf_op jit(solution)/shard_map/all_to_all | solution.py:83
  104.8 591.2 %all-reduce.3.cloned.1.call-start = ((), (), s32[]{:S(2)}) async-start(), calls=%async_computation.6 | async-start | bytes 663552 | tf_op jit(solution)/shard_map/psum | solution.py:93
Sparse Core Ops, SparseCore 0:
  29.3 37.3 all-gather.1
  69.5 55.4 reduce-scatter.3
  127.9 567.9 all-reduce.2
where the time goes:
time: 705 us; the launch traced here: 704 us
  waiting for transfers between devices  604 us (86%)
  blocking collectives  39.7 us (6%)
  starting transfers between devices  17.7 us (3%)
  local copies, waits for them, and re-layouts  14.3 us (2%)
  between operations  14 us (2%)
  other arithmetic  8.15 us (1%)
    psum x1, waiting for transfers between devices, on_device(): summed_all = lax.psum(partial_value, 'seq')  568 us
    all_to_all x1, blocking collectives, on_device(): lax.all_to_all(grad_frames_in, 'seq', split_axis=2, concat_axis=1, tiled=...  22.7 us
    unnamed x4, waiting for transfers between devices  20.9 us
    all_to_all x1, blocking collectives, on_device(): lax.all_to_all(mixed_pos, 'seq', split_axis=1, concat_axis=2, tiled=True)  17 us
    all_to_all x1, waiting for transfers between devices, on_device(): lax.all_to_all(qkv, 'seq', split_axis=2, concat_axis=1, tiled=True)  14.2 us
  transfers between devices with their start and end apart: 5, of which 3 were waited for; matrix products, arithmetic and copies ran while one was open for 3% of the time, Pallas kernels for 0%

commit v1 on v0

v1 whole, which is shorter than its diff:
```python
import math

import jax
import jax.numpy as jnp
from jax import lax
from jax.experimental import pallas as pl
from jax.experimental.pallas import tpu as pltpu
from jax.sharding import PartitionSpec as P

HEAD_DIM = 72
HEADS = 8
NX, NY, NZ = 4, 8, 8
MESH = pl.DeviceIdType.MESH
BF, F32 = jnp.bfloat16, jnp.float32


def place():
    dp, seq = lax.axis_index("dp"), lax.axis_index("seq")
    zh, core = dp // 2, dp % 2
    zl, y, x = seq // 32, (seq // 4) % 8, seq % 4
    return zh, core, zl, y, x


def device(zh, core, zl, y, x):
    return (zh * 2 + core, zl * 32 + y * 4 + x)


def peers():
    zh, core, zl, y, x = place()

    def at_core():
        return device(zh, 1 - core, zl, y, x)

    def at_x(r):
        return device(zh, core, zl, y, (x + r) % NX)

    def at_y(r):
        return device(zh, core, zl, (y + r) % NY, x)

    def at_z(r):
        z = (zh * 2 + zl + r) % NZ
        return device(z // 2, core, z % 2, y, x)

    def at_plane(r):
        return device(zh, core, zl, (y + r // NX) % NY, (x + r % NX) % NX)

    return at_core, at_x, at_y, at_z, at_plane


def weight_kernel(
    mixed_ref, up_ref, out_ref,
    own0, snd0, rcv0, snd1, rcv1, own1, snd2, rcv2, own2, snd3, rcv3, snd4, rcv4,
    s0, r0, s1, r1, s2, r2, s3, r3, s4, r4,
):
    zh, core, zl, y, x = place()
    at_core, at_x, at_y, at_z, at_plane = peers()

    barrier = pltpu.get_barrier_semaphore()
    pl.semaphore_signal(barrier, inc=1, device_id=at_core(), device_id_type=MESH)

    @pl.loop(1, NZ)
    def _(r):
        pl.semaphore_signal(barrier, inc=1, device_id=at_z(r), device_id_type=MESH)

    @pl.loop(1, NX * NY)
    def _(r):
        pl.semaphore_signal(barrier, inc=1, device_id=at_plane(r), device_id_type=MESH)

    def units(head, dst):
        rows = mixed_ref[head]
        for g in range(9):
            part = jnp.dot(
                rows, up_ref[:, g * 128:(g + 1) * 128], preferred_element_type=F32
            )
            yield g, part

    @pl.loop(0, 4)
    def _(h):
        for g, part in units(2 * h + 1 - core, snd0):
            for rb in range(9):
                u = rb * 9 + g
                snd0[u // 24, (u % 24) // 3, h, u % 3] = part[rb * 8:rb * 8 + 8].astype(BF)
        for u in range(81, 96):
            snd0[u // 24, (u % 24) // 3, h, u % 3] = jnp.zeros((8, 128), BF)

    pl.semaphore_wait(barrier, 1 + (NZ - 1) + (NX * NY - 1))

    copy0 = pltpu.make_async_remote_copy(
        src_ref=snd0, dst_ref=rcv0, send_sem=s0, recv_sem=r0,
        device_id=at_core(), device_id_type=MESH,
    )
    copy0.start()

    @pl.loop(0, 4)
    def _(h):
        for g, part in units(2 * h + core, own0):
            for rb in range(9):
                u = rb * 9 + g
                own0[u // 24, (u % 24) // 3, h, u % 3] = part[rb * 8:rb * 8 + 8]
        for u in range(81, 96):
            own0[u // 24, (u % 24) // 3, h, u % 3] = jnp.zeros((8, 128), F32)

    copy0.wait()

    def copy1(r):
        return pltpu.make_async_remote_copy(
            src_ref=snd1.at[r - 1], dst_ref=rcv1.at[r - 1],
            send_sem=s1.at[r - 1], recv_sem=r1.at[r - 1],
            device_id=at_x(r), device_id_type=MESH,
        )

    for r in (2, 1, 3):
        to = (x + r) % NX
        snd1[r - 1] = (own0[to] + rcv0[to].astype(F32)).astype(BF)
        copy1(r).start()
    own1[...] = own0[x] + rcv0[x].astype(F32)
    for r in (1, 3, 2):
        copy1(r).wait()
    own1[...] = (own1[...] + rcv1[0].astype(F32)) + (rcv1[1].astype(F32) + rcv1[2].astype(F32))

    def copy2(r):
        return pltpu.make_async_remote_copy(
            src_ref=snd2.at[r - 1], dst_ref=rcv2.at[r - 1],
            send_sem=s2.at[r - 1], recv_sem=r2.at[r - 1],
            device_id=at_y(r), device_id_type=MESH,
        )

    for r in (4, 3, 5, 2, 6, 1, 7):
        snd2[r - 1] = own1[(y + r) % NY].astype(BF)
        copy2(r).start()
    for r in (1, 7, 2, 6, 3, 5, 4):
        copy2(r).wait()
    total = own1[y]
    for r in range(NY - 1):
        total = total + rcv2[r].astype(F32)
    own2[...] = total

    def copy3(r):
        return pltpu.make_async_remote_copy(
            src_ref=snd3.at[r - 1], dst_ref=rcv3.at[r - 1],
            send_sem=s3.at[r - 1], recv_sem=r3.at[r - 1],
            device_id=at_z(r), device_id_type=MESH,
        )

    for r in (4, 3, 5, 2, 6, 1, 7):
        z = (zh * 2 + zl + r) % NZ
        snd3[r - 1] = own2[z // 2].astype(BF)
        copy3(r).start()
    for r in (1, 7, 2, 6, 3, 5, 4):
        copy3(r).wait()
    total = own2[zh]
    for r in range(NZ - 1):
        total = total + rcv3[r].astype(F32)
    snd4[...] = (total * (1.0 / 256.0)).astype(BF)

    me = x * NY + y

    def copy4(r):
        return pltpu.make_async_remote_copy(
            src_ref=snd4, dst_ref=rcv4.at[me],
            send_sem=s4, recv_sem=r4,
            device_id=at_plane(r), device_id_type=MESH,
        )

    @pl.loop(1, NX * NY)
    def _(r):
        copy4(r).start()

    keep = pltpu.make_async_copy(snd4, rcv4.at[me], r4)
    keep.start()
    pltpu.make_async_copy(rcv4, rcv4, r4).wait()
    sent = rcv4.at[pl.ds(0, NX * NY - 1)]
    pltpu.make_async_copy(sent, sent, s4).wait()
    for u in range(81):
        rb, g = u // 9, u % 9
        out_ref[rb * 8:rb * 8 + 8, g * 128:(g + 1) * 128] = rcv4[u // 3, u % 3].astype(F32)


def weight_sum(mixed_t, up):
    unit = (8, 128)
    vm = pltpu.VMEM
    dma = pltpu.SemaphoreType.DMA
    return pl.pallas_call(
        weight_kernel,
        out_shape=jax.ShapeDtypeStruct((HEAD_DIM, up.shape[1]), F32),
        in_specs=[pl.BlockSpec(memory_space=pltpu.VMEM)] * 2,
        out_specs=pl.BlockSpec(memory_space=pltpu.VMEM),
        scratch_shapes=[
            vm((4, 8, 4, 3) + unit, F32),
            vm((4, 8, 4, 3) + unit, BF),
            vm((4, 8, 4, 3) + unit, BF),
            vm((3, 8, 4, 3) + unit, BF),
            vm((3, 8, 4, 3) + unit, BF),
            vm((8, 4, 3) + unit, F32),
            vm((7, 4, 3) + unit, BF),
            vm((7, 4, 3) + unit, BF),
            vm((4, 3) + unit, F32),
            vm((7, 3) + unit, BF),
            vm((7, 3) + unit, BF),
            vm((3,) + unit, BF),
            vm((32, 3) + unit, BF),
            dma, dma,
            dma((3,)), dma((3,)),
            dma((7,)), dma((7,)),
            dma((7,)), dma((7,)),
            dma, dma,
        ],
        compiler_params=pltpu.CompilerParams(collective_id=1, has_side_effects=True),
        name="weight_sum",
    )(mixed_t, up)


def attend_all(stacked, grad_in, allowed, factor):
    frame_count, pos_here, _ = stacked.shape
    split = stacked.reshape(frame_count, pos_here, 3, HEADS, HEAD_DIM)
    queries, keys, values = split[:, :, 0], split[:, :, 1], split[:, :, 2]
    scores = jnp.einsum("fphd,gphd->phfg", queries, keys, preferred_element_type=F32) * factor
    scores = jnp.where(allowed, scores, F32(-1e30))
    exponent = jnp.exp(scores - jnp.max(scores, axis=-1, keepdims=True))
    attend = exponent / jnp.sum(exponent, axis=-1, keepdims=True)
    low = attend.astype(BF)
    mixed = jnp.einsum("phfg,gphd->fphd", low, values, preferred_element_type=F32).astype(BF)
    grad = grad_in.reshape(frame_count, pos_here, HEADS, HEAD_DIM)
    attend_grad = jnp.einsum("fphd,gphd->phfg", grad, values, preferred_element_type=F32)
    row_dot = jnp.sum(attend * attend_grad, axis=-1, keepdims=True)
    score_grad = (attend * (attend_grad - row_dot)).astype(BF)
    query_grad = (
        jnp.einsum("phfg,gphd->fphd", score_grad, keys, preferred_element_type=F32) * factor
    ).astype(BF)
    key_grad = (
        jnp.einsum("phfg,fphd->gphd", score_grad, queries, preferred_element_type=F32) * factor
    ).astype(BF)
    value_grad = jnp.einsum("phfg,fphd->gphd", low, grad, preferred_element_type=F32).astype(BF)
    packed = jnp.stack([query_grad, key_grad, value_grad], axis=2)
    return mixed, packed.reshape(frame_count, pos_here, 3 * HEADS * HEAD_DIM)


def on_device(qkv, segment_ids, upstream, out_weight):
    _, _, positions, packed = qkv.shape
    inner = HEADS * HEAD_DIM
    factor = 1.0 / math.sqrt(HEAD_DIM)
    full_weight = lax.all_gather(out_weight, "dp", axis=0, tiled=True)
    width = full_weight.shape[1]
    frames = lax.axis_size("seq")
    pos_here = positions // frames
    allowed = (segment_ids[0, :, None] == segment_ids[0, None, :])[None, None]

    both = jnp.concatenate([qkv, upstream], axis=-1).reshape(frames, pos_here, packed + width)
    both = lax.all_to_all(both, "seq", split_axis=0, concat_axis=0, tiled=True)
    stacked, up = both[..., :packed], both[..., packed:].reshape(frames * pos_here, width)

    grad_in = lax.dot_general(
        up, full_weight, (((1,), (1,)), ((), ())), preferred_element_type=F32
    ).astype(BF)
    mixed, packed_grad = attend_all(stacked, grad_in, allowed, factor)
    mixed_flat = mixed.reshape(frames * pos_here, inner)
    weight_grad = weight_sum(mixed_flat.T.reshape(HEADS, HEAD_DIM, -1), up)

    back = jnp.concatenate([packed_grad, mixed.reshape(frames, pos_here, inner)], axis=-1)
    back = lax.all_to_all(back, "seq", split_axis=0, concat_axis=0, tiled=True)
    back = back.reshape(positions, packed + inner)
    qkv_grad = back[:, :packed].reshape(qkv.shape)
    output = jnp.dot(back[:, packed:], full_weight, preferred_element_type=F32).astype(BF)
    return (output.reshape(upstream.shape), qkv_grad, weight_grad)


def solution(mesh):
    in_specs = (
        P("dp", "seq", None, None),
        P("dp", None),
        P("dp", "seq", None, None),
        P("dp", None),
    )
    out_specs = (P("dp", "seq", None, None), P("dp", "seq", None, None), P("dp", None))
    return jax.shard_map(
        on_device, mesh=mesh, in_specs=in_specs, out_specs=out_specs, check_vma=False
    )
```

time: 705 us -> 137 us (0.19)
  the two profiles are of different devices: /device:TPU:64 before, /device:TPU:1 now
where the time goes in v1:
time: 137 us; the launch traced here: 136 us
  Pallas kernels  42.2 us (31%)
  waiting for transfers between devices  37.2 us (27%)
  starting transfers between devices  24.1 us (18%)
  between operations  14.3 us (10%)
  local copies, waits for them, and re-layouts  11.6 us (8%)
  matrix products  4.67 us (3%)
  other arithmetic  2.44 us (2%)
    pallas_call x1, Pallas kernels, weight_sum(): pl.pallas_call(weight_kernel, out_shape=jax.ShapeDtypeStruct((HEAD_DIM, u...  42.2 us
    all_to_all x1, waiting for transfers between devices, on_device(): both = lax.all_to_all(both, 'seq', split_axis=0, concat_axis=0, tiled=True)  19.8 us
    all_gather x1, waiting for transfers between devices, on_device(): full_weight = lax.all_gather(out_weight, 'dp', axis=0, tiled=True)  16.7 us
    all_to_all x1, starting transfers between devices, on_device(): both = lax.all_to_all(both, 'seq', split_axis=0, concat_axis=0, tiled=True)  12.9 us
    all_to_all x1, starting transfers between devices, on_device(): back = lax.all_to_all(back, 'seq', split_axis=0, concat_axis=0, tiled=True)  11.1 us
    unnamed x11, local copies, waits for them, and re-layouts  2.93 us
  transfers between devices with their start and end apart: 3, of which 2 were waited for; matrix products, arithmetic and copies ran while one was open for 4% of the time, Pallas kernels for 31%

profile of v1, /device:TPU:1, one launch (start us, length us, event | category | flops | bytes accessed | tf_op | source)
XLA Modules:
  0.0 136.5 jit_solution(4791554157132377783)
XLA Ops:
  7.2 1.2 copy.30
  8.3 1.1 pad_maximum_fusion.1
  9.4 0.3 copy.31
  9.8 0.0 copy-start.3
  9.8 1.2 reshape.72
  11.0 12.9 %all-to-all-start = ((bf16[64,2,2880]{2,1,0:T(2,128)(2,1)}), bf16[64,2,2880]{2,1,0:T(2,128)(2,1)S(1)}, u32[]{:S(2)}, u32[]{:S(2)}) async-start(bf16[64,2,2880]{2,1,0:T(2,128)(2,1)} %reshape.72), calls=%async_computation | async-start | bytes 1507328 | tf_op jit(solution)/shard_map/all_to_all | solution.py:249
  23.9 0.0 all-gather.2.cloned.1.call-start
  24.0 0.7 all-gather.2.cloned.1.call-update
  24.7 0.1 broadcast_compare_fusion
  24.7 19.8 %all-to-all-done = bf16[64,2,2880]{2,1,0:T(2,128)(2,1)S(1)} async-done(((bf16[64,2,2880]{2,1,0:T(2,128)(2,1)}), bf16[64,2,2880]{2,1,0:T(2,128)(2,1)S(1)}, u32[]{:S(2)}, u32[]{:S(2)}) %all-to-all-start) | async-done | bytes 737312 | tf_op jit(solution)/shard_map/all_to_all | solution.py:249
  44.6 0.5 slice.31
  45.0 0.1 reshape.74.up_ref
  45.2 0.0 copy-start.1
  45.2 0.3 slice.28
  45.5 1.4 reshape.83
  46.9 0.1 fusion.17
  47.0 0.3 fusion.4
  47.3 0.9 fusion.18
  48.2 0.3 fusion.10
  48.5 0.2 copy.42
  48.7 0.2 reshape.77
  48.9 16.7 %all-gather.2.cloned.1.call-done = bf16[576,1152]{1,0:T(8,128)(2,1)} async-done(((bf16[72,1152]{1,0:T(8,128)(2,1)}), bf16[576,1152]{1,0:T(8,128)(2,1)}) %all-gather.2.cloned.1.call-update) | async-done | bytes 1327120 | tf_op jit(solution)/shard_map/all_gather | solution.py:242
  65.6 0.0 copy-done.1
  65.6 1.8 %convolution_convert_fusion.3 = bf16[128,576]{0,1:T(8,128)(2,1)S(1)} fusion(bf16[128,1152]{1,0:T(8,128)(2,1)S(1)} %reshape.74.up_ref, bf16[576,1152]{1,0:T(8,128)(2,1)} %all-gather.2.cloned.1.call-done), kind=kOutput, calls=%fused_computation.17 | convolution fusion | flops 169943040 | bytes 1769472 | tf_op jit(solution)/shard_map/dot_general | solution.py:252
  67.4 0.2 copy.35
  67.6 0.3 reshape.75
  67.8 0.3 fusion.9
  68.1 0.3 multiply_reduce_fusion
  68.4 0.1 multiply_convert_fusion
  68.5 0.2 fusion.7
  68.8 0.3 fusion.8
  69.0 0.2 pad_maximum_fusion
  69.2 0.5 copy.40
  69.8 0.5 reshape.76
  70.3 0.1 pad_maximum_fusion.2
  70.4 1.4 %copy.43 = bf16[64,2,2304]{2,1,0:T(2,128)(2,1)} copy(bf16[64,2,2304]{2,0,1:T(8,128)(2,1)S(1)} %pad_maximum_fusion.2) | data formatting | bytes 1179648 | tf_op jit(solution)/shard_map/concatenate | solution.py:259
  71.9 11.1 %all-to-all-start.1 = ((bf16[64,2,2304]{2,1,0:T(2,128)(2,1)}), bf16[64,2,2304]{2,1,0:T(2,128)(2,1)S(1)}, u32[]{:S(2)}, u32[]{:S(2)}) async-start(bf16[64,2,2304]{2,1,0:T(2,128)(2,1)} %copy.43), calls=%async_computation.1 | async-start | bytes 1179648 | tf_op jit(solution)/shard_map/all_to_all | solution.py:260
  83.0 0.2 copy.44
  83.2 0.2 reshape.81
  83.4 0.8 copy.45
  84.2 42.2 %weight_sum.1 = f32[72,1152]{1,0:T(8,128)} custom-call(bf16[8,72,128]{2,1,0:T(8,128)(2,1)} %bitcast.56, bf16[128,1152]{1,0:T(8,128)(2,1)} %copy-done.1), custom_call_target="tpu_custom_call" | custom-call | tf_op jit(solution)/shard_map/weight_sum/pallas_call | solution.py:183
  126.4 0.0 copy-start
  126.4 0.0 all-to-all-done.1
  126.4 0.2 reshape.78
  126.7 1.0 copy.46
  127.6 0.1 copy-done
  127.7 1.2 fusion.1
  128.9 0.7 copy.72
  (4 shorter events, 0.0 us)
Async XLA Ops:
  9.8 14.9 %copy-start.3 = (s32[1,64]{1,0:T(1,128)S(1)}, s32[1,64]{1,0:T(1,128)}, u32[]{:S(2)}) copy-start(s32[1,64]{1,0:T(1,128)} %param.5) | copy-start | bytes 772
  11.0 33.6 %all-to-all-start = ((bf16[64,2,2880]{2,1,0:T(2,128)(2,1)}), bf16[64,2,2880]{2,1,0:T(2,128)(2,1)S(1)}, u32[]{:S(2)}, u32[]{:S(2)}) async-start(bf16[64,2,2880]{2,1,0:T(2,128)(2,1)} %reshape.72), calls=%async_computation | async-start | bytes 1507328 | tf_op jit(solution)/shard_map/all_to_all | solution.py:249
  23.9 41.6 %all-gather.2.cloned.1.call-start = ((), (), s32[]{:S(2)}) async-start(), calls=%async_computation.2 | async-start | bytes 1492992 | tf_op jit(solution)/shard_map/all_gather | solution.py:242
  45.2 20.4 %copy-start.1 = (bf16[128,1152]{1,0:T(8,128)(2,1)}, bf16[128,1152]{1,0:T(8,128)(2,1)S(1)}, u32[]{:S(2)}) copy-start(bf16[128,1152]{1,0:T(8,128)(2,1)S(1)} %reshape.74.up_ref) | copy-start | bytes 884740
  71.9 54.5 %all-to-all-start.1 = ((bf16[64,2,2304]{2,1,0:T(2,128)(2,1)}), bf16[64,2,2304]{2,1,0:T(2,128)(2,1)S(1)}, u32[]{:S(2)}, u32[]{:S(2)}) async-start(bf16[64,2,2304]{2,1,0:T(2,128)(2,1)} %copy.43), calls=%async_computation.1 | async-start | bytes 1179648 | tf_op jit(solution)/shard_map/all_to_all | solution.py:260
  126.4 1.3 copy-start
  126.7 2.2 %copy-start.2 = (f32[72,1152]{1,0:T(8,128)S(1)}, f32[72,1152]{1,0:T(8,128)}, u32[]{:S(2)}) copy-start(f32[72,1152]{1,0:T(8,128)} %weight_sum.1) | copy-start | bytes 995332
Sparse Core Ops, SparseCore 0:
  26.9 38.5 all-gather.1

commit v2 on v1

--- a/solution.py
+++ b/solution.py
@@ -44,27 +44,164 @@
     def at_plane(r):
         return device(zh, core, zl, (y + r // NX) % NY, (x + r % NX) % NX)
 
-    return at_core, at_x, at_y, at_z, at_plane
-
-
-def weight_kernel(
-    mixed_ref, up_ref, out_ref,
+    def at_seq(r):
+        return device(zh, core, (zl + r // 32) % 2, (y + r // NX) % NY, (x + r % NX) % NX)
+
+    return at_core, at_x, at_y, at_z, at_plane, at_seq
+
+
+def exchange(src, dst, send_sem, recv_sem, keep_sem):
+    _, _, _, _, _, at_seq = peers()
+    me = lax.axis_index("seq")
+
+    def start(r):
+        to = at_seq(r)
+        pltpu.make_async_remote_copy(
+            src_ref=src.at[to[1]], dst_ref=dst.at[me], send_sem=send_sem, recv_sem=recv_sem,
+            device_id=to, device_id_type=MESH,
+        ).start()
+
+    def keep():
+        return pltpu.make_async_copy(src.at[me], dst.at[me], keep_sem)
+
+    def finish():
+        keep().wait()
+        others = dst.at[pl.ds(0, NX * NY * 2 - 1)]
+        pltpu.make_async_copy(others, others, recv_sem).wait()
+        pltpu.make_async_copy(others, others, send_sem).wait()
+
+    return start, keep, finish
+
+
+def greet(barrier):
+    at_core, _, _, at_z, _, at_seq = peers()
+    pl.semaphore_signal(barrier, inc=1, device_id=at_core(), device_id_type=MESH)
+
+    @pl.loop(1, NZ)
+    def _(r):
+        pl.semaphore_signal(barrier, inc=1, device_id=at_z(r), device_id_type=MESH)
+
+    @pl.loop(1, NX * NY * 2)
+    def _(r):
+        pl.semaphore_signal(barrier, inc=1, device_id=at_seq(r), device_id_type=MESH)
+
+
+GREETED = 1 + (NZ - 1) + (NX * NY * 2 - 1)
+
+
+def enter_kernel(
+    qkv_ref, up_ref, w_ref, qkv_out, up_out, w_out,
+    qs, qr, qk, us, ur, uk, wk, os, orr, zs, zr, xs, xr, cs, cr, ds, dr,
+):
+    zh, core, zl, y, x = place()
+    dp = zh * 2 + core
+    at_core = peers()[0]
+    barrier = pltpu.get_barrier_semaphore()
+    greet(barrier)
+    q_start, q_keep, q_finish = exchange(qkv_ref, qkv_out, qs, qr, qk)
+    u_start, u_keep, u_finish = exchange(up_ref, up_out, us, ur, uk)
+    q_keep().start()
+    u_keep().start()
+    w_keep = pltpu.make_async_copy(w_ref, w_out.at[dp], wk)
+    w_keep.start()
+    pl.semaphore_wait(barrier, GREETED)
+
+    def remote(src, dst, ss, rs, to):
+        return pltpu.make_async_remote_copy(
+            src_ref=src, dst_ref=dst, send_sem=ss, recv_sem=rs,
+            device_id=to, device_id_type=MESH,
+        )
+
+    def over_z(r, part):
+        to = device((zh + r) % 4, core, zl, y, x)
+        return remote(w_ref.at[part], w_out.at[dp, part], zs.at[r - 1], zr.at[r - 1], to)
+
+    def landed(r, part, sem):
+        ref = w_out.at[((zh + 4 - r) % 4) * 2 + core, part]
+        pltpu.make_async_copy(ref, ref, sem).wait()
+        return ref
+
+    def landed_core(r, part, sem):
+        ref = w_out.at[((zh + 4 - r) % 4) * 2 + 1 - core, part]
+        pltpu.make_async_copy(ref, ref, sem).wait()
+
+    halves = (pl.ds(0, 5), pl.ds(5, 4))
+    own_core = remote(w_ref, w_out.at[dp], os, orr, at_core())
+    for half in (0, 1):
+        @pl.when(x % 2 == half)
+        def _(half=half):
+            for r in (2, 1, 3):
+                over_z(r, halves[half]).start()
+
+    own_core.start()
+
+    @pl.loop(1, NX * NY * 2)
+    def _(r):
+        q_start(NX * NY * 2 - r)
+
+    @pl.loop(1, NX * NY * 2)
+    def _(r):
+        u_start(NX * NY * 2 - r)
+
+    across = device(zh, core, zl, y, x + 1 - 2 * (x % 2))
+    for half in (0, 1):
+        @pl.when(x % 2 == half)
+        def _(half=half):
+            mine, other = halves[half], halves[1 - half]
+            for r in (1, 3, 2):
+                ref = landed(r, mine, zr.at[r - 1])
+                remote(ref, ref, xs.at[r - 1], xr.at[r - 1], across).start()
+                remote(ref, ref, cs.at[r - 1], cr.at[r - 1], at_core()).start()
+            for r in (1, 3, 2):
+                ref = landed(r, other, xr.at[r - 1])
+                remote(ref, ref, ds.at[r - 1], dr.at[r - 1], at_core()).start()
+            for r in (1, 3, 2):
+                over_z(r, mine).wait_send()
+                landed(r, mine, xs.at[r - 1])
+                landed(r, mine, cs.at[r - 1])
+                landed(r, other, ds.at[r - 1])
+                landed_core(r, mine, cr.at[r - 1])
+                landed_core(r, other, dr.at[r - 1])
+
+    own_core.wait()
+    w_keep.wait()
+    q_finish()
+    u_finish()
+
+
+def enter(qkv, up, weight):
+    dma = pltpu.SemaphoreType.DMA
+    spec = pl.BlockSpec(memory_space=pltpu.VMEM)
+    return pl.pallas_call(
+        enter_kernel,
+        out_shape=[
+            jax.ShapeDtypeStruct(qkv.shape, BF),
+            jax.ShapeDtypeStruct(up.shape, BF),
+            jax.ShapeDtypeStruct((HEADS,) + weight.shape, BF),
+        ],
+        in_specs=[spec] * 3,
+        out_specs=[spec] * 3,
+        scratch_shapes=[dma] * 9 + [dma((3,))] * 8,
+        compiler_params=pltpu.CompilerParams(collective_id=0, has_side_effects=True),
+        name="enter",
+    )(qkv, up, weight)
+
+
+def leave_kernel(
+    grad_ref, back_ref, mixed_ref, up_ref, grad_out, back_out, out_ref,
+    gs, gr, gk, bs, br, bk,
     own0, snd0, rcv0, snd1, rcv1, own1, snd2, rcv2, own2, snd3, rcv3, snd4, rcv4,
     s0, r0, s1, r1, s2, r2, s3, r3, s4, r4,
 ):
     zh, core, zl, y, x = place()
-    at_core, at_x, at_y, at_z, at_plane = peers()
+    at_core, at_x, at_y, at_z, at_plane, _ = peers()
 
     barrier = pltpu.get_barrier_semaphore()
-    pl.semaphore_signal(barrier, inc=1, device_id=at_core(), device_id_type=MESH)
-
-    @pl.loop(1, NZ)
-    def _(r):
-        pl.semaphore_signal(barrier, inc=1, device_id=at_z(r), device_id_type=MESH)
-
-    @pl.loop(1, NX * NY)
-    def _(r):
-        pl.semaphore_signal(barrier, inc=1, device_id=at_plane(r), device_id_type=MESH)
+    greet(barrier)
+    g_start, g_keep, g_finish = exchange(grad_ref, grad_out, gs, gr, gk)
+    b_start, b_keep, b_finish = exchange(back_ref, back_out, bs, br, bk)
+    g_keep().start()
+    b_keep().start()
 
     def units(head, dst):
         rows = mixed_ref[head]
@@ -83,13 +220,21 @@
         for u in range(81, 96):
             snd0[u // 24, (u % 24) // 3, h, u % 3] = jnp.zeros((8, 128), BF)
 
-    pl.semaphore_wait(barrier, 1 + (NZ - 1) + (NX * NY - 1))
+    pl.semaphore_wait(barrier, GREETED)
 
     copy0 = pltpu.make_async_remote_copy(
         src_ref=snd0, dst_ref=rcv0, send_sem=s0, recv_sem=r0,
         device_id=at_core(), device_id_type=MESH,
     )
     copy0.start()
+
+    @pl.loop(1, NX * NY * 2)
+    def _(r):
+        g_start(NX * NY * 2 - r)
+
+    @pl.loop(1, NX * NY * 2)
+    def _(r):
+        b_start(NX * NY * 2 - r)
 
     @pl.loop(0, 4)
     def _(h):
@@ -174,18 +319,24 @@
     for u in range(81):
         rb, g = u // 9, u % 9
         out_ref[rb * 8:rb * 8 + 8, g * 128:(g + 1) * 128] = rcv4[u // 3, u % 3].astype(F32)
-
-
-def weight_sum(mixed_t, up):
+    g_finish()
+    b_finish()
+
+
+def leave(grad, back, mixed_t, up):
     unit = (8, 128)
     vm = pltpu.VMEM
     dma = pltpu.SemaphoreType.DMA
     return pl.pallas_call(
-        weight_kernel,
-        out_shape=jax.ShapeDtypeStruct((HEAD_DIM, up.shape[1]), F32),
-        in_specs=[pl.BlockSpec(memory_space=pltpu.VMEM)] * 2,
-        out_specs=pl.BlockSpec(memory_space=pltpu.VMEM),
-        scratch_shapes=[
+        leave_kernel,
+        out_shape=[
+            jax.ShapeDtypeStruct(grad.shape, BF),
+            jax.ShapeDtypeStruct(back.shape, BF),
+            jax.ShapeDtypeStruct((HEAD_DIM, up.shape[1]), F32),
+        ],
+        in_specs=[pl.BlockSpec(memory_space=pltpu.VMEM)] * 4,
+        out_specs=[pl.BlockSpec(memory_space=pltpu.VMEM)] * 3,
+        scratch_shapes=[dma] * 6 + [
             vm((4, 8, 4, 3) + unit, F32),
             vm((4, 8, 4, 3) + unit, BF),
             vm((4, 8, 4, 3) + unit, BF),
@@ -206,8 +357,8 @@
             dma, dma,
         ],
         compiler_params=pltpu.CompilerParams(collective_id=1, has_side_effects=True),
-        name="weight_sum",
-    )(mixed_t, up)
+        name="leave",
+    )(grad, back, mixed_t, up)
 
 
 def attend_all(stacked, grad_in, allowed, factor):
@@ -239,29 +390,30 @@
     _, _, positions, packed = qkv.shape
     inner = HEADS * HEAD_DIM
     factor = 1.0 / math.sqrt(HEAD_DIM)
-    full_weight = lax.all_gather(out_weight, "dp", axis=0, tiled=True)
-    width = full_weight.shape[1]
+    width = out_weight.shape[1]
     frames = lax.axis_size("seq")
     pos_here = positions // frames
     allowed = (segment_ids[0, :, None] == segment_ids[0, None, :])[None, None]
 
-    both = jnp.concatenate([qkv, upstream], axis=-1).reshape(frames, pos_here, packed + width)
-    both = lax.all_to_all(both, "seq", split_axis=0, concat_axis=0, tiled=True)
-    stacked, up = both[..., :packed], both[..., packed:].reshape(frames * pos_here, width)
+    stacked, up, full_weight = enter(
+        qkv.reshape(frames, pos_here, packed),
+        upstream.reshape(frames, pos_here, width),
+        out_weight.reshape(HEAD_DIM // 8, 8, width),
+    )
+    full_weight = full_weight.reshape(inner, width)
+    up = up.reshape(frames * pos_here, width)
 
     grad_in = lax.dot_general(
         up, full_weight, (((1,), (1,)), ((), ())), preferred_element_type=F32
     ).astype(BF)
     mixed, packed_grad = attend_all(stacked, grad_in, allowed, factor)
-    mixed_flat = mixed.reshape(frames * pos_here, inner)
-    weight_grad = weight_sum(mixed_flat.T.reshape(HEADS, HEAD_DIM, -1), up)
-
-    back = jnp.concatenate([packed_grad, mixed.reshape(frames, pos_here, inner)], axis=-1)
-    back = lax.all_to_all(back, "seq", split_axis=0, concat_axis=0, tiled=True)
-    back = back.reshape(positions, packed + inner)
-    qkv_grad = back[:, :packed].reshape(qkv.shape)
-    output = jnp.dot(back[:, packed:], full_weight, preferred_element_type=F32).astype(BF)
-    return (output.reshape(upstream.shape), qkv_grad, weight_grad)
+    mixed_t = mixed.reshape(frames * pos_here, inner).T.reshape(HEADS, HEAD_DIM, -1)
+    back = mixed.reshape(frames, pos_here, inner)
+    qkv_grad, back, weight_grad = leave(packed_grad, back, mixed_t, up)
+    output = jnp.dot(
+        back.reshape(positions, inner), full_weight, preferred_element_type=F32
+    ).astype(BF)
+    return (output.reshape(upstream.shape), qkv_grad.reshape(qkv.shape), weight_grad)
 
 
 def solution(mesh):

time: 137 us -> 113 us (0.82)
  Pallas kernels: 42.2 us -> 88.8 us
  waiting for transfers between devices: 37.2 us -> 0 us
  starting transfers between devices: 24.1 us -> 0 us
  between operations: 14.3 us -> 0.83 us
  local copies, waits for them, and re-layouts: 11.6 us -> 15.2 us
    pallas_call x1 -> x2, Pallas kernels: 42.2 us -> 88.8 us  [the longest x1 44.6 us: leave(): pl.pallas_call(leave_kernel, out_shape=[jax.ShapeDtypeStruct(grad.shape,...]
    all_to_all x2 -> x0, starting transfers between devices: 24.1 us -> none  [the longest x1 12.9 us: on_device(): both = lax.all_to_all(both, 'seq', split_axis=0, concat_axis=0, tiled=True)]
    all_to_all x2 -> x0, waiting for transfers between devices: 19.8 us -> none  [the longest x1 19.8 us: on_device(): both = lax.all_to_all(both, 'seq', split_axis=0, concat_axis=0, tiled=True)]
    all_gather x1 -> x0, waiting for transfers between devices: 16.7 us -> none  [on_device(): full_weight = lax.all_gather(out_weight, 'dp', axis=0, tiled=True)]
    reshape x6 -> x7, local copies, waits for them, and re-layouts: 1.98 us -> 6.63 us  [the longest x1 1.79 us: on_device(): upstream.reshape(frames, pos_here, width)]
    concatenate x2 -> x0, local copies, waits for them, and re-layouts: 1.8 us -> none  [the longest x1 1.45 us: on_device(): jnp.concatenate([packed_grad, mixed.reshape(frames, pos_here, inner)], ax...]
    reshape x1, local copies, waits for them, and re-layouts: 0.54 us -> 2.2 us  [attend_all(): return (mixed, packed.reshape(frame_count, pos_here, 3 * HEADS * HEAD_DIM))]
    unnamed x11 -> x13, local copies, waits for them, and re-layouts: 2.93 us -> 2.93 us
  transfers between devices with their start and end apart: 3 -> 0, of which waited for: 2 -> 0; matrix products, arithmetic and copies ran while one was open for 4% -> 0% of each run, Pallas kernels for 31% -> 0%
where the time goes in v2:
time: 113 us; the launch traced here: 112 us
  Pallas kernels  88.8 us (79%)
  local copies, waits for them, and re-layouts  15.2 us (13%)
  matrix products  4.72 us (4%)
  other arithmetic  1.99 us (2%)
    pallas_call x1, Pallas kernels, leave(): pl.pallas_call(leave_kernel, out_shape=[jax.ShapeDtypeStruct(grad.shape,...  44.6 us
    pallas_call x1, Pallas kernels, enter(): pl.pallas_call(enter_kernel, out_shape=[jax.ShapeDtypeStruct(qkv.shape, B...  44.2 us
    unnamed x13, local copies, waits for them, and re-layouts  2.93 us

profile of v2, /device:TPU:1, one launch (start us, length us, event | category | flops | bytes accessed | tf_op | source)
XLA Modules:
  0.0 111.5 jit_solution(16036766681810926602)
XLA Ops:
  0.6 0.8 broadcast_compare_fusion
  1.4 1.8 %reshape.82.up_ref = bf16[64,2,1152]{2,1,0:T(2,128)(2,1)} reshape(bf16[1,1,128,1152]{3,2,1,0:T(8,128)(2,1)} %param.6) | data formatting | bytes 589824 | tf_op jit(solution)/shard_map/reshape | solution.py:400
  3.2 1.2 %copy.18 = bf16[1,1,128,1728]{3,2,1,0:T(8,128)(2,1)S(1)} copy(bf16[1,1,128,1728]{2,3,1,0:T(8,128)(2,1)} %param.4) | data formatting | bytes 884736 | tf_op args[0]
  4.4 1.0 reshape.81.qkv_ref
  5.4 44.2 %enter.1 = (bf16[64,2,1728]{2,1,0:T(2,128)(2,1)}, bf16[64,2,1152]{2,1,0:T(2,128)(2,1)}, bf16[8,9,8,1152]{3,2,1,0:T(8,128)(2,1)}) custom-call(bf16[64,2,1728]{2,1,0:T(2,128)(2,1)} %reshape.81.qkv_ref, bf16[64,2,1152]{2,1,0:T(2,128)(2,1)} %reshape.82.up_ref, bf16[9,8,1152]{2,1,0:T(8,128)(2,1)} %bitcast.58), custom_call_target="tpu_custom_call" | custom-call | tf_op jit(solution)/shard_map/enter/pallas_call | solution.py:175
  49.7 1.1 reshape.85.up_ref
  50.7 0.0 copy-start.1
  50.8 0.0 copy-start.3
  50.8 1.9 %convolution_convert_fusion.3 = bf16[128,576]{0,1:T(8,128)(2,1)S(1)} fusion(bf16[128,1152]{1,0:T(8,128)(2,1)S(1)} %reshape.85.up_ref, bf16[576,1152]{1,0:T(8,128)(2,1)} %bitcast.54), kind=kOutput, calls=%fused_computation.17 | convolution fusion | flops 169943040 | bytes 1769472 | tf_op jit(solution)/shard_map/dot_general | solution.py:406
  52.7 0.2 copy.21
  52.9 0.3 reshape.87
  53.2 0.0 copy-done.3
  53.2 1.4 %reshape.84 = bf16[64,2,3,8,72]{4,3,2,1,0:T(8,128)(2,1)S(1)} reshape(bf16[64,2,1728]{2,1,0:T(2,128)(2,1)S(1)} %copy-done.3) | data formatting | bytes 884736 | tf_op jit(solution)/shard_map/reshape | solution.py:366
  54.5 0.0 copy-done.1
  54.5 0.1 fusion.16
  54.7 0.3 fusion.4
  55.0 0.9 fusion.17
  55.9 0.3 fusion.9
  56.2 0.3 fusion.10
  56.5 0.2 copy.28
  56.7 0.3 multiply_reduce_fusion
  57.0 0.1 multiply_convert_fusion
  57.1 0.2 fusion.7
  57.3 0.3 fusion.8
  57.6 0.2 pad_maximum_fusion
  57.8 0.5 copy.26
  58.3 2.2 %reshape.88.grad_ref = bf16[64,2,1728]{2,1,0:T(2,128)(2,1)} reshape(bf16[64,2,3,8,72]{4,3,2,1,0:T(8,128)(2,1)S(1)} %copy.26) | data formatting | bytes 884736 | tf_op jit(solution)/shard_map/reshape | solution.py:386
  60.5 0.0 copy-start
  60.5 0.2 reshape.90
  60.7 1.2 %reshape.89.back_ref = bf16[64,2,576]{2,1,0:T(2,128)(2,1)} reshape(bf16[64,2,8,72]{3,2,1,0:T(8,128)(2,1)S(1)} %copy.28) | data formatting | bytes 294912 | tf_op jit(solution)/shard_map/reshape | solution.py:411
  61.9 0.8 copy.30
  62.6 44.6 %leave.1 = (bf16[64,2,1728]{2,1,0:T(2,128)(2,1)}, bf16[64,2,576]{2,1,0:T(2,128)(2,1)}, f32[72,1152]{1,0:T(8,128)}) custom-call(bf16[64,2,1728]{2,1,0:T(2,128)(2,1)} %reshape.88.grad_ref, bf16[64,2,576]{2,1,0:T(2,128)(2,1)} %reshape.89.back_ref, bf16[8,72,128]{2,1,0:T(8,128)(2,1)} %bitcast.57, bf16[128,1152]{1,0:T(8,128)(2,1)} %copy-done.1), custom_call_target="tpu_custom_call" | custom-call | tf_op jit(solution)/shard_map/leave/pallas_call | solution.py:330
  107.2 0.0 copy-start.2
  107.2 1.1 reshape.92
  108.3 0.0 copy-done
  108.3 1.1 %fusion.1 = bf16[1,1,128,1152]{3,2,1,0:T(8,128)(2,1)} fusion(bf16[128,576]{1,0:T(8,128)(2,1)S(1)} %reshape.92, bf16[576,1152]{1,0:T(8,128)(2,1)S(1)} %bitcast.55), kind=kOutput, calls=%fused_computation.2 | convolution fusion | flops 170016768 | bytes 1769472 | tf_op jit(solution)/shard_map/dot_general | solution.py:413
  109.5 0.0 copy-done.2
  109.5 0.0 copy-start.4
  109.5 0.3 reshape.94
  109.8 1.0 copy.31
  110.8 0.0 copy-done.4
  110.8 0.7 copy.55
Async XLA Ops:
  50.7 3.8 %copy-start.1 = (bf16[128,1152]{1,0:T(8,128)(2,1)}, bf16[128,1152]{1,0:T(8,128)(2,1)S(1)}, u32[]{:S(2)}) copy-start(bf16[128,1152]{1,0:T(8,128)(2,1)S(1)} %reshape.85.up_ref) | copy-start | bytes 884740
  50.8 2.4 %copy-start.3 = (bf16[64,2,1728]{2,1,0:T(2,128)(2,1)S(1)}, bf16[64,2,1728]{2,1,0:T(2,128)(2,1)}, u32[]{:S(2)}) copy-start(bf16[64,2,1728]{2,1,0:T(2,128)(2,1)} %get-tuple-element.9) | copy-start | bytes 1327108
  60.5 47.8 %copy-start = (bf16[8,9,8,1152]{3,2,1,0:T(8,128)(2,1)S(1)}, bf16[8,9,8,1152]{3,2,1,0:T(8,128)(2,1)}, u32[]{:S(2)}) copy-start(bf16[8,9,8,1152]{3,2,1,0:T(8,128)(2,1)} %get-tuple-element.11) | copy-start | bytes 3981316
  107.2 2.2 %copy-start.2 = (bf16[64,2,1728]{2,1,0:T(2,128)(2,1)S(1)}, bf16[64,2,1728]{2,1,0:T(2,128)(2,1)}, u32[]{:S(2)}) copy-start(bf16[64,2,1728]{2,1,0:T(2,128)(2,1)} %get-tuple-element.13) | copy-start | bytes 1327108
  109.5 1.3 %copy-start.4 = (f32[72,1152]{1,0:T(8,128)S(1)}, f32[72,1152]{1,0:T(8,128)}, u32[]{:S(2)}) copy-start(f32[72,1152]{1,0:T(8,128)} %get-tuple-element.33) | copy-start | bytes 995332

commit v3 on v2

--- a/solution.py
+++ b/solution.py
@@ -44,8 +44,10 @@
     def at_plane(r):
         return device(zh, core, zl, (y + r // NX) % NY, (x + r % NX) % NX)
 
-    def at_seq(r):
-        return device(zh, core, (zl + r // 32) % 2, (y + r // NX) % NY, (x + r % NX) % NX)
+    def at_seq(k):
+        i, c = k % 8, k // 8
+        dy = 4 + (i // 2) * (1 - 2 * (i % 2)) - i % 2
+        return device(zh, core, (zl + c // 4 + i) % 2, (y + dy) % NY, (x + c + i) % NX)
 
     return at_core, at_x, at_y, at_z, at_plane, at_seq
 
@@ -81,9 +83,9 @@
     def _(r):
         pl.semaphore_signal(barrier, inc=1, device_id=at_z(r), device_id_type=MESH)
 
-    @pl.loop(1, NX * NY * 2)
-    def _(r):
-        pl.semaphore_signal(barrier, inc=1, device_id=at_seq(r), device_id_type=MESH)
+    @pl.loop(48, 48 + 63)
+    def _(k):
+        pl.semaphore_signal(barrier, inc=1, device_id=at_seq(k % 64), device_id_type=MESH)
 
 
 GREETED = 1 + (NZ - 1) + (NX * NY * 2 - 1)
@@ -135,14 +137,13 @@
 
     own_core.start()
 
-    @pl.loop(1, NX * NY * 2)
-    def _(r):
-        q_start(NX * NY * 2 - r)
-
-    @pl.loop(1, NX * NY * 2)
-    def _(r):
-        u_start(NX * NY * 2 - r)
-
+    def send_in(low, high):
+        @pl.loop(48 + low, 48 + high)
+        def _(k):
+            q_start(k % 64)
+            u_start(k % 64)
+
+    send_in(0, 63)
     across = device(zh, core, zl, y, x + 1 - 2 * (x % 2))
     for half in (0, 1):
         @pl.when(x % 2 == half)
@@ -152,6 +153,11 @@
                 ref = landed(r, mine, zr.at[r - 1])
                 remote(ref, ref, xs.at[r - 1], xr.at[r - 1], across).start()
                 remote(ref, ref, cs.at[r - 1], cr.at[r - 1], at_core()).start()
+
+    for half in (0, 1):
+        @pl.when(x % 2 == half)
+        def _(half=half):
+            mine, other = halves[half], halves[1 - half]
             for r in (1, 3, 2):
                 ref = landed(r, other, xr.at[r - 1])
                 remote(ref, ref, ds.at[r - 1], dr.at[r - 1], at_core()).start()
@@ -190,8 +196,8 @@
 def leave_kernel(
     grad_ref, back_ref, mixed_ref, up_ref, grad_out, back_out, out_ref,
     gs, gr, gk, bs, br, bk,
-    own0, snd0, rcv0, snd1, rcv1, own1, snd2, rcv2, own2, snd3, rcv3, snd4, rcv4,
-    s0, r0, s1, r1, s2, r2, s3, r3, s4, r4,
+    own0, rows0, cols0, snd1, rcv1, own1, snd2, rcv2, own2, snd3, rcv3, snd4, rcv4,
+    s0, r0, t0, q0, s1, r1, s2, r2, s3, r3, s4, r4,
 ):
     zh, core, zl, y, x = place()
     at_core, at_x, at_y, at_z, at_plane, _ = peers()
@@ -203,49 +209,46 @@
     g_keep().start()
     b_keep().start()
 
-    def units(head, dst):
-        rows = mixed_ref[head]
+    def add(rows, cols, first):
         for g in range(9):
             part = jnp.dot(
-                rows, up_ref[:, g * 128:(g + 1) * 128], preferred_element_type=F32
+                rows[...], cols[:, g * 128:(g + 1) * 128], preferred_element_type=F32
             )
-            yield g, part
-
-    @pl.loop(0, 4)
-    def _(h):
-        for g, part in units(2 * h + 1 - core, snd0):
-            for rb in range(9):
-                u = rb * 9 + g
-                snd0[u // 24, (u % 24) // 3, h, u % 3] = part[rb * 8:rb * 8 + 8].astype(BF)
-        for u in range(81, 96):
-            snd0[u // 24, (u % 24) // 3, h, u % 3] = jnp.zeros((8, 128), BF)
-
-    pl.semaphore_wait(barrier, GREETED)
-
-    copy0 = pltpu.make_async_remote_copy(
-        src_ref=snd0, dst_ref=rcv0, send_sem=s0, recv_sem=r0,
-        device_id=at_core(), device_id_type=MESH,
-    )
-    copy0.start()
-
-    @pl.loop(1, NX * NY * 2)
-    def _(r):
-        g_start(NX * NY * 2 - r)
-
-    @pl.loop(1, NX * NY * 2)
-    def _(r):
-        b_start(NX * NY * 2 - r)
-
-    @pl.loop(0, 4)
-    def _(h):
-        for g, part in units(2 * h + core, own0):
-            for rb in range(9):
-                u = rb * 9 + g
-                own0[u // 24, (u % 24) // 3, h, u % 3] = part[rb * 8:rb * 8 + 8]
+            for h in range(4):
+                for rb in range(9):
+                    u, at = rb * 9 + g, h * HEAD_DIM + rb * 8
+                    spot = (u // 24, (u % 24) // 3, h, u % 3)
+                    unit = part[at:at + 8]
+                    own0[spot] = unit if first else own0[spot] + unit
+
+    add(mixed_ref.at[core], up_ref, True)
+    for h in range(4):
         for u in range(81, 96):
             own0[u // 24, (u % 24) // 3, h, u % 3] = jnp.zeros((8, 128), F32)
-
-    copy0.wait()
+    pl.semaphore_wait(barrier, GREETED)
+
+    def to_core(src, dst, ss, rs):
+        return pltpu.make_async_remote_copy(
+            src_ref=src, dst_ref=dst, send_sem=ss, recv_sem=rs,
+            device_id=at_core(), device_id_type=MESH,
+        )
+
+    trade = (
+        to_core(mixed_ref.at[1 - core], rows0, s0, r0),
+        to_core(up_ref, cols0, t0, q0),
+    )
+    for copy in trade:
+        copy.start()
+
+    def send_back(low, high):
+        @pl.loop(48 + low, 48 + high)
+        def _(k):
+            g_start(k % 64)
+            b_start(k % 64)
+
+    for copy in trade:
+        copy.wait()
+    add(rows0, cols0, False)
 
     def copy1(r):
         return pltpu.make_async_remote_copy(
@@ -256,9 +259,10 @@
 
     for r in (2, 1, 3):
         to = (x + r) % NX
-        snd1[r - 1] = (own0[to] + rcv0[to].astype(F32)).astype(BF)
+        snd1[r - 1] = own0[to].astype(BF)
         copy1(r).start()
-    own1[...] = own0[x] + rcv0[x].astype(F32)
+    send_back(0, 32)
+    own1[...] = own0[x]
     for r in (1, 3, 2):
         copy1(r).wait()
     own1[...] = (own1[...] + rcv1[0].astype(F32)) + (rcv1[1].astype(F32) + rcv1[2].astype(F32))
@@ -273,6 +277,7 @@
     for r in (4, 3, 5, 2, 6, 1, 7):
         snd2[r - 1] = own1[(y + r) % NY].astype(BF)
         copy2(r).start()
+    send_back(32, 48)
     for r in (1, 7, 2, 6, 3, 5, 4):
         copy2(r).wait()
     total = own1[y]
@@ -291,6 +296,7 @@
         z = (zh * 2 + zl + r) % NZ
         snd3[r - 1] = own2[z // 2].astype(BF)
         copy3(r).start()
+    send_back(48, 63)
     for r in (1, 7, 2, 6, 3, 5, 4):
         copy3(r).wait()
     total = own2[zh]
@@ -316,9 +322,9 @@
     pltpu.make_async_copy(rcv4, rcv4, r4).wait()
     sent = rcv4.at[pl.ds(0, NX * NY - 1)]
     pltpu.make_async_copy(sent, sent, s4).wait()
-    for u in range(81):
-        rb, g = u // 9, u % 9
-        out_ref[rb * 8:rb * 8 + 8, g * 128:(g + 1) * 128] = rcv4[u // 3, u % 3].astype(F32)
+    result = pltpu.make_async_copy(rcv4, out_ref, s4)
+    result.start()
+    result.wait()
     g_finish()
     b_finish()
 
@@ -332,14 +338,14 @@
         out_shape=[
             jax.ShapeDtypeStruct(grad.shape, BF),
             jax.ShapeDtypeStruct(back.shape, BF),
-            jax.ShapeDtypeStruct((HEAD_DIM, up.shape[1]), F32),
+            jax.ShapeDtypeStruct((32, 3, 8, 128), BF),
         ],
         in_specs=[pl.BlockSpec(memory_space=pltpu.VMEM)] * 4,
         out_specs=[pl.BlockSpec(memory_space=pltpu.VMEM)] * 3,
         scratch_shapes=[dma] * 6 + [
             vm((4, 8, 4, 3) + unit, F32),
-            vm((4, 8, 4, 3) + unit, BF),
-            vm((4, 8, 4, 3) + unit, BF),
+            vm((4 * HEAD_DIM, up.shape[0]), BF),
+            vm(up.shape, BF),
             vm((3, 8, 4, 3) + unit, BF),
             vm((3, 8, 4, 3) + unit, BF),
             vm((8, 4, 3) + unit, F32),
@@ -350,7 +356,7 @@
             vm((7, 3) + unit, BF),
             vm((3,) + unit, BF),
             vm((32, 3) + unit, BF),
-            dma, dma,
+            dma, dma, dma, dma,
             dma((3,)), dma((3,)),
             dma((7,)), dma((7,)),
             dma((7,)), dma((7,)),
@@ -393,13 +399,13 @@
     width = out_weight.shape[1]
     frames = lax.axis_size("seq")
     pos_here = positions // frames
-    allowed = (segment_ids[0, :, None] == segment_ids[0, None, :])[None, None]
-
     stacked, up, full_weight = enter(
         qkv.reshape(frames, pos_here, packed),
         upstream.reshape(frames, pos_here, width),
         out_weight.reshape(HEAD_DIM // 8, 8, width),
     )
+    stacked, segment_ids = lax.optimization_barrier((stacked, segment_ids))
+    allowed = (segment_ids[0, :, None] == segment_ids[0, None, :])[None, None]
     full_weight = full_weight.reshape(inner, width)
     up = up.reshape(frames * pos_here, width)
 
@@ -407,9 +413,12 @@
         up, full_weight, (((1,), (1,)), ((), ())), preferred_element_type=F32
     ).astype(BF)
     mixed, packed_grad = attend_all(stacked, grad_in, allowed, factor)
-    mixed_t = mixed.reshape(frames * pos_here, inner).T.reshape(HEADS, HEAD_DIM, -1)
+    mixed_t = mixed.reshape(frames * pos_here, HEADS // 2, 2, HEAD_DIM)
+    mixed_t = mixed_t.transpose(2, 1, 3, 0).reshape(2, inner // 2, frames * pos_here)
     back = mixed.reshape(frames, pos_here, inner)
-    qkv_grad, back, weight_grad = leave(packed_grad, back, mixed_t, up)
+    qkv_grad, back, units = leave(packed_grad, back, mixed_t, up)
+    units = units.reshape(96, 8, 128)[:81].reshape(9, 9, 8, 128)
+    weight_grad = units.transpose(0, 2, 1, 3).reshape(HEAD_DIM, width).astype(F32)
     output = jnp.dot(
         back.reshape(positions, inner), full_weight, preferred_element_type=F32
     ).astype(BF)

time: 113 us -> 110 us (0.973); the launches traced: 112 us -> 110 us
    pallas_call x1, Pallas kernels: 44.2 us -> 42.6 us  [enter(): pl.pallas_call(enter_kernel, out_shape=[jax.ShapeDtypeStruct(qkv.shape, B...]
    unnamed x13 -> x14, local copies, waits for them, and re-layouts: 2.93 us -> 2.22 us
where the time goes in v3:
time: 110 us
  Pallas kernels  88 us (80%)
  local copies, waits for them, and re-layouts  14.3 us (13%)
  matrix products  4.72 us (4%)
  other arithmetic  2.01 us (2%)
    pallas_call x1, Pallas kernels, leave(): pl.pallas_call(leave_kernel, out_shape=[jax.ShapeDtypeStruct(grad.shape,...  45.4 us
    pallas_call x1, Pallas kernels, enter(): pl.pallas_call(enter_kernel, out_shape=[jax.ShapeDtypeStruct(qkv.shape, B...  42.6 us
    unnamed x14, local copies, waits for them, and re-layouts  2.22 us
    reshape x1, local copies, waits for them, and re-layouts, attend_all(): return (mixed, packed.reshape(frame_count, pos_here, 3 * HEADS * HEAD_DIM))  2.2 us

profile of v3, /device:TPU:1, one launch (start us, length us, event | category | flops | bytes accessed | tf_op | source)
XLA Modules:
  0.0 109.9 jit_solution(10304524186045308080)
XLA Ops:
  0.6 1.8 %reshape.91.up_ref = bf16[64,2,1152]{2,1,0:T(2,128)(2,1)} reshape(bf16[1,1,128,1152]{3,2,1,0:T(8,128)(2,1)} %param.6) | data formatting | bytes 589824 | tf_op jit(solution)/shard_map/reshape | solution.py:404
  2.4 0.0 copy-start.5
  2.4 1.2 %copy.18 = bf16[1,1,128,1728]{3,2,1,0:T(8,128)(2,1)S(1)} copy(bf16[1,1,128,1728]{2,3,1,0:T(8,128)(2,1)} %param.4) | data formatting | bytes 884736 | tf_op args[0]
  3.7 1.0 reshape.90.qkv_ref
  4.6 42.6 %enter.1 = (bf16[64,2,1728]{2,1,0:T(2,128)(2,1)}, bf16[64,2,1152]{2,1,0:T(2,128)(2,1)}, bf16[8,9,8,1152]{3,2,1,0:T(8,128)(2,1)}) custom-call(bf16[64,2,1728]{2,1,0:T(2,128)(2,1)} %reshape.90.qkv_ref, bf16[64,2,1152]{2,1,0:T(2,128)(2,1)} %reshape.91.up_ref, bf16[9,8,1152]{2,1,0:T(8,128)(2,1)} %bitcast.67), custom_call_target="tpu_custom_call" | custom-call | tf_op jit(solution)/shard_map/enter/pallas_call | solution.py:181
  47.3 0.0 copy-done.5
  47.3 0.1 broadcast_compare_fusion
  47.4 1.1 reshape.94.up_ref
  48.4 0.0 copy-start.1
  48.4 0.0 copy-start.3
  48.5 1.9 %convolution_convert_fusion.3 = bf16[128,576]{0,1:T(8,128)(2,1)S(1)} fusion(bf16[128,1152]{1,0:T(8,128)(2,1)S(1)} %reshape.94.up_ref, bf16[576,1152]{1,0:T(8,128)(2,1)} %bitcast.62), kind=kOutput, calls=%fused_computation.17 | convolution fusion | flops 169943040 | bytes 1769472 | tf_op jit(solution)/shard_map/dot_general | solution.py:412
  50.4 0.2 copy.21
  50.6 0.3 reshape.96
  50.9 0.0 copy-done.3
  50.9 1.4 %reshape.93 = bf16[64,2,3,8,72]{4,3,2,1,0:T(8,128)(2,1)S(1)} reshape(bf16[64,2,1728]{2,1,0:T(2,128)(2,1)S(1)} %copy-done.3) | data formatting | bytes 884736 | tf_op jit(solution)/shard_map/reshape | solution.py:372
  52.2 0.0 copy-done.1
  52.2 0.1 fusion.16
  52.4 0.3 fusion.4
  52.7 0.9 fusion.17
  53.6 0.3 fusion.9
  53.8 0.3 fusion.10
  54.2 0.2 copy.28
  54.3 0.3 multiply_reduce_fusion
  54.6 0.1 multiply_convert_fusion
  54.8 0.2 fusion.7
  55.0 0.3 fusion.8
  55.3 0.2 pad_maximum_fusion
  55.5 0.5 copy.26
  56.0 2.2 %reshape.97.grad_ref = bf16[64,2,1728]{2,1,0:T(2,128)(2,1)} reshape(bf16[64,2,3,8,72]{4,3,2,1,0:T(8,128)(2,1)S(1)} %copy.26) | data formatting | bytes 884736 | tf_op jit(solution)/shard_map/reshape | solution.py:392
  58.2 0.0 copy-start
  58.2 0.8 copy.30
  59.0 1.2 %reshape.98.back_ref = bf16[64,2,576]{2,1,0:T(2,128)(2,1)} reshape(bf16[64,2,8,72]{3,2,1,0:T(8,128)(2,1)S(1)} %copy.28) | data formatting | bytes 294912 | tf_op jit(solution)/shard_map/reshape | solution.py:418
  60.2 45.4 %leave.1 = (bf16[64,2,1728]{2,1,0:T(2,128)(2,1)}, bf16[64,2,576]{2,1,0:T(2,128)(2,1)}, bf16[32,3,8,128]{3,2,1,0:T(8,128)(2,1)}) custom-call(bf16[64,2,1728]{2,1,0:T(2,128)(2,1)} %reshape.97.grad_ref, bf16[64,2,576]{2,1,0:T(2,128)(2,1)} %reshape.98.back_ref, bf16[2,288,128]{2,1,0:T(8,128)(2,1)} %bitcast.66, bf16[128,1152]{1,0:T(8,128)(2,1)} %copy-done.1), custom_call_target="tpu_custom_call" | custom-call | tf_op jit(solution)/shard_map/leave/pallas_call | solution.py:336
  105.5 0.0 copy-start.4
  105.5 1.1 reshape.101
  106.6 0.0 copy-done
  106.6 0.0 copy-start.2
  106.6 1.1 %fusion.1 = bf16[1,1,128,1152]{3,2,1,0:T(8,128)(2,1)} fusion(bf16[128,576]{1,0:T(8,128)(2,1)S(1)} %reshape.101, bf16[576,1152]{1,0:T(8,128)(2,1)S(1)} %bitcast.63), kind=kOutput, calls=%fused_computation.2 | convolution fusion | flops 170016768 | bytes 1769472 | tf_op jit(solution)/shard_map/dot_general | solution.py:422
  107.8 0.0 copy-done.4
  107.8 0.7 convert_bitcast_fusion
  108.5 0.0 copy-done.2
  108.5 0.3 reshape.103
  108.9 1.0 copy.31
  (1 shorter events, 0.0 us)
Async XLA Ops:
  2.4 44.9 %copy-start.5 = (s32[1,64]{1,0:T(1,128)S(1)}, s32[1,64]{1,0:T(1,128)}, u32[]{:S(2)}) copy-start(s32[1,64]{1,0:T(1,128)} %param.5) | copy-start | bytes 772
  48.4 3.8 %copy-start.1 = (bf16[128,1152]{1,0:T(8,128)(2,1)}, bf16[128,1152]{1,0:T(8,128)(2,1)S(1)}, u32[]{:S(2)}) copy-start(bf16[128,1152]{1,0:T(8,128)(2,1)S(1)} %reshape.94.up_ref) | copy-start | bytes 884740
  48.4 2.4 %copy-start.3 = (bf16[64,2,1728]{2,1,0:T(2,128)(2,1)S(1)}, bf16[64,2,1728]{2,1,0:T(2,128)(2,1)}, u32[]{:S(2)}) copy-start(bf16[64,2,1728]{2,1,0:T(2,128)(2,1)} %get-tuple-element.12) | copy-start | bytes 1327108
  58.2 48.4 %copy-start = (bf16[8,9,8,1152]{3,2,1,0:T(8,128)(2,1)S(1)}, bf16[8,9,8,1152]{3,2,1,0:T(8,128)(2,1)}, u32[]{:S(2)}) copy-start(bf16[8,9,8,1152]{3,2,1,0:T(8,128)(2,1)} %get-tuple-element.15) | copy-start | bytes 3981316
  105.5 2.2 %copy-start.4 = (bf16[32,3,8,128]{3,2,1,0:T(8,128)(2,1)S(1)}, bf16[32,3,8,128]{3,2,1,0:T(8,128)(2,1)}, u32[]{:S(2)}) copy-start(bf16[32,3,8,128]{3,2,1,0:T(8,128)(2,1)} %get-tuple-element.18) | copy-start | bytes 589828
  106.6 1.9 %copy-start.2 = (bf16[64,2,1728]{2,1,0:T(2,128)(2,1)S(1)}, bf16[64,2,1728]{2,1,0:T(2,128)(2,1)}, u32[]{:S(2)}) copy-start(bf16[64,2,1728]{2,1,0:T(2,128)(2,1)} %get-tuple-element.17) | copy-start | bytes 1327108

commit v4 on v3

--- a/solution.py
+++ b/solution.py
@@ -92,8 +92,8 @@
 
 
 def enter_kernel(
-    qkv_ref, up_ref, w_ref, qkv_out, up_out, w_out,
-    qs, qr, qk, us, ur, uk, wk, os, orr, zs, zr, xs, xr, cs, cr, ds, dr,
+    qkv_in, up_in, w_ref, qkv_out, up_out, w_out,
+    qkv_ref, up_ref, qs, qr, qk, us, ur, uk, wk, os, orr, zs, zr, xs, xr, cs, cr, ds, dr,
 ):
     zh, core, zl, y, x = place()
     dp = zh * 2 + core
@@ -102,6 +102,8 @@
     greet(barrier)
     q_start, q_keep, q_finish = exchange(qkv_ref, qkv_out, qs, qr, qk)
     u_start, u_keep, u_finish = exchange(up_ref, up_out, us, ur, uk)
+    up_ref[...] = up_in[...].reshape(up_ref.shape)
+    qkv_ref[...] = qkv_in[...].T.reshape(qkv_ref.shape)
     q_keep().start()
     u_keep().start()
     w_keep = pltpu.make_async_copy(w_ref, w_out.at[dp], wk)
@@ -175,27 +177,30 @@
     u_finish()
 
 
-def enter(qkv, up, weight):
+def enter(qkv, up, weight, frames):
     dma = pltpu.SemaphoreType.DMA
     spec = pl.BlockSpec(memory_space=pltpu.VMEM)
+    qkv_shape = (frames, qkv.shape[1] // frames, qkv.shape[0])
+    up_shape = (frames, up.shape[0] // frames, up.shape[1])
     return pl.pallas_call(
         enter_kernel,
         out_shape=[
-            jax.ShapeDtypeStruct(qkv.shape, BF),
-            jax.ShapeDtypeStruct(up.shape, BF),
+            jax.ShapeDtypeStruct(qkv_shape, BF),
+            jax.ShapeDtypeStruct(up_shape, BF),
             jax.ShapeDtypeStruct((HEADS,) + weight.shape, BF),
         ],
         in_specs=[spec] * 3,
         out_specs=[spec] * 3,
-        scratch_shapes=[dma] * 9 + [dma((3,))] * 8,
+        scratch_shapes=[pltpu.VMEM(qkv_shape, BF), pltpu.VMEM(up_shape, BF)]
+        + [dma] * 9 + [dma((3,))] * 8,
         compiler_params=pltpu.CompilerParams(collective_id=0, has_side_effects=True),
         name="enter",
     )(qkv, up, weight)
 
 
 def leave_kernel(
-    grad_ref, back_ref, mixed_ref, up_ref, grad_out, back_out, out_ref,
-    gs, gr, gk, bs, br, bk,
+    grad_in, back_in, mixed_ref, up_ref, grad_out, back_out, out_ref,
+    grad_ref, back_ref, gs, gr, gk, bs, br, bk,
     own0, rows0, cols0, snd1, rcv1, own1, snd2, rcv2, own2, snd3, rcv3, snd4, rcv4,
     s0, r0, t0, q0, s1, r1, s2, r2, s3, r3, s4, r4,
 ):
@@ -206,6 +211,9 @@
     greet(barrier)
     g_start, g_keep, g_finish = exchange(grad_ref, grad_out, gs, gr, gk)
     b_start, b_keep, b_finish = exchange(back_ref, back_out, bs, br, bk)
+    for p in range(grad_in.shape[0]):
+        back_ref[:, p, :] = back_in[p]
+        grad_ref[:, p, :] = grad_in[p]
     g_keep().start()
     b_keep().start()
 
@@ -331,18 +339,20 @@
 
 def leave(grad, back, mixed_t, up):
     unit = (8, 128)
+    grad_shape = (grad.shape[1], grad.shape[0], grad.shape[2])
+    back_shape = (back.shape[1], back.shape[0], back.shape[2])
     vm = pltpu.VMEM
     dma = pltpu.SemaphoreType.DMA
     return pl.pallas_call(
         leave_kernel,
         out_shape=[
-            jax.ShapeDtypeStruct(grad.shape, BF),
-            jax.ShapeDtypeStruct(back.shape, BF),
+            jax.ShapeDtypeStruct(grad_shape, BF),
+            jax.ShapeDtypeStruct(back_shape, BF),
             jax.ShapeDtypeStruct((32, 3, 8, 128), BF),
         ],
         in_specs=[pl.BlockSpec(memory_space=pltpu.VMEM)] * 4,
         out_specs=[pl.BlockSpec(memory_space=pltpu.VMEM)] * 3,
-        scratch_shapes=[dma] * 6 + [
+        scratch_shapes=[vm(grad_shape, BF), vm(back_shape, BF)] + [dma] * 6 + [
             vm((4, 8, 4, 3) + unit, F32),
             vm((4 * HEAD_DIM, up.shape[0]), BF),
             vm(up.shape, BF),
@@ -388,8 +398,8 @@
         jnp.einsum("phfg,fphd->gphd", score_grad, queries, preferred_element_type=F32) * factor
     ).astype(BF)
     value_grad = jnp.einsum("phfg,fphd->gphd", low, grad, preferred_element_type=F32).astype(BF)
-    packed = jnp.stack([query_grad, key_grad, value_grad], axis=2)
-    return mixed, packed.reshape(frame_count, pos_here, 3 * HEADS * HEAD_DIM)
+    packed = jnp.stack([query_grad, key_grad, value_grad], axis=2).transpose(1, 0, 2, 3, 4)
+    return mixed, packed.reshape(pos_here, frame_count, 3 * HEADS * HEAD_DIM)
 
 
 def on_device(qkv, segment_ids, upstream, out_weight):
@@ -400,9 +410,10 @@
     frames = lax.axis_size("seq")
     pos_here = positions // frames
     stacked, up, full_weight = enter(
-        qkv.reshape(frames, pos_here, packed),
-        upstream.reshape(frames, pos_here, width),
+        qkv.reshape(positions, packed).T,
+        upstream.reshape(positions, width),
         out_weight.reshape(HEAD_DIM // 8, 8, width),
+        frames,
     )
     stacked, segment_ids = lax.optimization_barrier((stacked, segment_ids))
     allowed = (segment_ids[0, :, None] == segment_ids[0, None, :])[None, None]
@@ -415,7 +426,7 @@
     mixed, packed_grad = attend_all(stacked, grad_in, allowed, factor)
     mixed_t = mixed.reshape(frames * pos_here, HEADS // 2, 2, HEAD_DIM)
     mixed_t = mixed_t.transpose(2, 1, 3, 0).reshape(2, inner // 2, frames * pos_here)
-    back = mixed.reshape(frames, pos_here, inner)
+    back = mixed.transpose(1, 0, 2, 3).reshape(pos_here, frames, inner)
     qkv_grad, back, units = leave(packed_grad, back, mixed_t, up)
     units = units.reshape(96, 8, 128)[:81].reshape(9, 9, 8, 128)
     weight_grad = units.transpose(0, 2, 1, 3).reshape(HEAD_DIM, width).astype(F32)

time: 110 us -> 106 us (0.964)
  local copies, waits for them, and re-layouts: 14.3 us -> 9.29 us
    reshape x4 -> x2, local copies, waits for them, and re-layouts: 6.12 us -> 2.18 us  [the longest x1 1.32 us: attend_all(): return (mixed, packed.reshape(pos_here, frame_count, 3 * HEADS * HEAD_DIM))]
    unnamed x14 -> x11, local copies, waits for them, and re-layouts: 2.22 us -> 0.99 us
where the time goes in v4:
time: 106 us; the launch traced here: 105 us
  Pallas kernels  87.9 us (83%)
  local copies, waits for them, and re-layouts  9.29 us (9%)
  matrix products  4.72 us (4%)
  other arithmetic  2.74 us (3%)
    pallas_call x1, Pallas kernels, leave(): pl.pallas_call(leave_kernel, out_shape=[jax.ShapeDtypeStruct(grad_shape,...  45.3 us
    pallas_call x1, Pallas kernels, enter(): pl.pallas_call(enter_kernel, out_shape=[jax.ShapeDtypeStruct(qkv_shape, B...  42.6 us

profile of v4, /device:TPU:1, one launch (start us, length us, event | category | flops | bytes accessed | tf_op | source)
XLA Modules:
  0.0 105.5 jit_solution(11610232363814988888)
XLA Ops:
  0.6 42.6 %enter.1 = (bf16[64,2,1728]{2,1,0:T(2,128)(2,1)}, bf16[64,2,1152]{2,1,0:T(2,128)(2,1)}, bf16[8,9,8,1152]{3,2,1,0:T(8,128)(2,1)}) custom-call(bf16[1728,128]{1,0:T(8,128)(2,1)} %bitcast.71, bf16[128,1152]{1,0:T(8,128)(2,1)} %bitcast.72, bf16[9,8,1152]{2,1,0:T(8,128)(2,1)} %bitcast.73), custom_call_target="tpu_custom_call" | custom-call | tf_op jit(solution)/shard_map/enter/pallas_call | solution.py:185
  43.3 0.8 broadcast_compare_fusion
  44.1 1.1 %reshape.94.up_ref = bf16[128,1152]{1,0:T(8,128)(2,1)S(1)} reshape(bf16[64,2,1152]{2,1,0:T(2,128)(2,1)} %get-tuple-element.14) | data formatting | bytes 589824 | tf_op jit(solution)/shard_map/reshape | solution.py:421
  45.1 0.0 copy-start.1
  45.2 0.0 copy-start.3
  45.2 1.9 %convolution_convert_fusion.3 = bf16[128,576]{0,1:T(8,128)(2,1)S(1)} fusion(bf16[128,1152]{1,0:T(8,128)(2,1)S(1)} %reshape.94.up_ref, bf16[576,1152]{1,0:T(8,128)(2,1)} %bitcast.64), kind=kOutput, calls=%fused_computation.16 | convolution fusion | flops 169943040 | bytes 1769472 | tf_op jit(solution)/shard_map/dot_general | solution.py:423
  47.1 0.2 copy.19
  47.3 0.3 reshape.96
  47.6 0.0 copy-done.3
  47.6 1.4 %reshape.93 = bf16[64,2,3,8,72]{4,3,2,1,0:T(8,128)(2,1)S(1)} reshape(bf16[64,2,1728]{2,1,0:T(2,128)(2,1)S(1)} %copy-done.3) | data formatting | bytes 884736 | tf_op jit(solution)/shard_map/reshape | solution.py:382
  48.9 0.0 copy-done.1
  49.0 0.1 fusion.15
  49.1 0.3 fusion.4
  49.4 0.9 fusion.16
  50.3 0.3 convolution_convert_fusion.1
  50.6 0.3 fusion.9
  50.9 0.3 multiply_reduce_fusion
  51.2 0.1 multiply_convert_fusion
  51.3 0.2 fusion.7
  51.5 0.3 fusion.8
  51.8 0.2 maximum_bitcast_fusion
  52.0 0.5 copy.24
  52.5 1.3 %reshape.97.grad_in = bf16[2,64,1728]{2,1,0:T(8,128)(2,1)} reshape(bf16[2,64,3,8,72]{4,3,2,1,0:T(8,128)(2,1)S(1)} %copy.24) | data formatting | bytes 884736 | tf_op jit(solution)/shard_map/reshape | solution.py:402
  53.8 0.2 copy.26
  54.0 0.0 copy-start
  54.0 0.9 reshape.98.back_in
  54.9 0.2 copy.27
  55.1 0.8 copy.28
  55.9 45.3 %leave.1 = (bf16[64,2,1728]{2,1,0:T(2,128)(2,1)}, bf16[64,2,576]{2,1,0:T(2,128)(2,1)}, bf16[32,3,8,128]{3,2,1,0:T(8,128)(2,1)}) custom-call(bf16[2,64,1728]{2,1,0:T(8,128)(2,1)} %reshape.97.grad_in, bf16[2,64,576]{2,1,0:T(8,128)(2,1)} %reshape.98.back_in, bf16[2,288,128]{2,1,0:T(8,128)(2,1)} %bitcast.70, bf16[128,1152]{1,0:T(8,128)(2,1)} %copy-done.1), custom_call_target="tpu_custom_call" | custom-call | tf_op jit(solution)/shard_map/leave/pallas_call | solution.py:346
  101.2 0.0 copy-start.4
  101.2 1.1 %reshape.101 = bf16[128,576]{1,0:T(8,128)(2,1)S(1)} reshape(bf16[64,2,576]{2,1,0:T(2,128)(2,1)} %get-tuple-element.16) | data formatting | bytes 294912 | tf_op jit(solution)/shard_map/reshape | solution.py:434
  102.2 0.0 copy-done
  102.3 0.0 copy-start.2
  102.3 1.1 %fusion.1 = bf16[1,1,128,1152]{3,2,1,0:T(8,128)(2,1)} fusion(bf16[128,576]{1,0:T(8,128)(2,1)S(1)} %reshape.101, bf16[576,1152]{1,0:T(8,128)(2,1)S(1)} %bitcast.65), kind=kOutput, calls=%fused_computation.2 | convolution fusion | flops 170016768 | bytes 1769472 | tf_op jit(solution)/shard_map/dot_general | solution.py:433
  103.4 0.0 copy-done.4
  103.4 0.7 convert_bitcast_fusion
  104.2 0.0 copy-done.2
  104.2 0.3 reshape.103
  104.5 1.0 copy.29
  (1 shorter events, 0.0 us)
Async XLA Ops:
  45.1 3.8 %copy-start.1 = (bf16[128,1152]{1,0:T(8,128)(2,1)}, bf16[128,1152]{1,0:T(8,128)(2,1)S(1)}, u32[]{:S(2)}) copy-start(bf16[128,1152]{1,0:T(8,128)(2,1)S(1)} %reshape.94.up_ref) | copy-start | bytes 884740
  45.2 2.4 %copy-start.3 = (bf16[64,2,1728]{2,1,0:T(2,128)(2,1)S(1)}, bf16[64,2,1728]{2,1,0:T(2,128)(2,1)}, u32[]{:S(2)}) copy-start(bf16[64,2,1728]{2,1,0:T(2,128)(2,1)} %get-tuple-element.12) | copy-start | bytes 1327108
  54.0 48.2 %copy-start = (bf16[8,9,8,1152]{3,2,1,0:T(8,128)(2,1)S(1)}, bf16[8,9,8,1152]{3,2,1,0:T(8,128)(2,1)}, u32[]{:S(2)}) copy-start(bf16[8,9,8,1152]{3,2,1,0:T(8,128)(2,1)} %get-tuple-element.15) | copy-start | bytes 3981316
  101.2 2.2 %copy-start.4 = (bf16[32,3,8,128]{3,2,1,0:T(8,128)(2,1)S(1)}, bf16[32,3,8,128]{3,2,1,0:T(8,128)(2,1)}, u32[]{:S(2)}) copy-start(bf16[32,3,8,128]{3,2,1,0:T(8,128)(2,1)} %get-tuple-element.18) | copy-start | bytes 589828
  102.3 1.9 %copy-start.2 = (bf16[64,2,1728]{2,1,0:T(2,128)(2,1)S(1)}, bf16[64,2,1728]{2,1,0:T(2,128)(2,1)}, u32[]{:S(2)}) copy-start(bf16[64,2,1728]{2,1,0:T(2,128)(2,1)} %get-tuple-element.17) | copy-start | bytes 1327108

commit v5 on v4

--- a/solution.py
+++ b/solution.py
@@ -92,14 +92,24 @@
 
 
 def enter_kernel(
-    qkv_in, up_in, w_ref, qkv_out, up_out, w_out,
-    qkv_ref, up_ref, qs, qr, qk, us, ur, uk, wk, os, orr, zs, zr, xs, xr, cs, cr, ds, dr,
+    qkv_hbm, up_hbm, w_hbm, qkv_out, up_out, w_out,
+    qkv_in, up_in, w_ref, load_sem, qkv_ref, up_ref, qs, qr, qk, us, ur, uk, wk, os, orr, zs, zr, xs, xr, cs, cr, ds, dr,
 ):
     zh, core, zl, y, x = place()
     dp = zh * 2 + core
     at_core = peers()[0]
     barrier = pltpu.get_barrier_semaphore()
+    loads = [
+        pltpu.make_async_copy(src, dst, load_sem.at[i])
+        for i, (src, dst) in enumerate(
+            ((up_hbm, up_in), (qkv_hbm, qkv_in), (w_hbm, w_ref))
+        )
+    ]
+    for load in loads:
+        load.start()
     greet(barrier)
+    for load in loads:
+        load.wait()
     q_start, q_keep, q_finish = exchange(qkv_ref, qkv_out, qs, qr, qk)
     u_start, u_keep, u_finish = exchange(up_ref, up_out, us, ur, uk)
     up_ref[...] = up_in[...].reshape(up_ref.shape)
@@ -189,9 +199,12 @@
             jax.ShapeDtypeStruct(up_shape, BF),
             jax.ShapeDtypeStruct((HEADS,) + weight.shape, BF),
         ],
-        in_specs=[spec] * 3,
+        in_specs=[pl.BlockSpec(memory_space=pltpu.HBM)] * 3,
         out_specs=[spec] * 3,
-        scratch_shapes=[pltpu.VMEM(qkv_shape, BF), pltpu.VMEM(up_shape, BF)]
+        scratch_shapes=[
+            pltpu.VMEM(qkv.shape, BF), pltpu.VMEM(up.shape, BF), pltpu.VMEM(weight.shape, BF),
+            dma((3,)),
+        ] + [pltpu.VMEM(qkv_shape, BF), pltpu.VMEM(up_shape, BF)]
         + [dma] * 9 + [dma((3,))] * 8,
         compiler_params=pltpu.CompilerParams(collective_id=0, has_side_effects=True),
         name="enter",
@@ -199,8 +212,8 @@
 
 
 def leave_kernel(
-    grad_in, back_in, mixed_ref, up_ref, grad_out, back_out, out_ref,
-    grad_ref, back_ref, gs, gr, gk, bs, br, bk,
+    grad_in, back_in, mixed_ref, up_ref, w_ref, grad_res, res_ref, out_ref,
+    grad_ref, back_ref, grad_out, back_out, gs, gr, gk, bs, br, bk,
     own0, rows0, cols0, snd1, rcv1, own1, snd2, rcv2, own2, snd3, rcv3, snd4, rcv4,
     s0, r0, t0, q0, s1, r1, s2, r2, s3, r3, s4, r4,
 ):
@@ -327,17 +340,23 @@
 
     keep = pltpu.make_async_copy(snd4, rcv4.at[me], r4)
     keep.start()
+    b_finish()
+    flat = back_out[...].reshape(res_ref.shape[0], w_ref.shape[0])
+    for g in range(0, 1152, 384):
+        res_ref[:, g:g + 384] = jnp.dot(
+            flat, w_ref[:, g:g + 384], preferred_element_type=F32
+        ).astype(BF)
+    g_finish()
+    grad_res[...] = grad_out[...].reshape(grad_res.shape[1], grad_res.shape[0]).T
     pltpu.make_async_copy(rcv4, rcv4, r4).wait()
     sent = rcv4.at[pl.ds(0, NX * NY - 1)]
     pltpu.make_async_copy(sent, sent, s4).wait()
     result = pltpu.make_async_copy(rcv4, out_ref, s4)
     result.start()
     result.wait()
-    g_finish()
-    b_finish()
-
-
-def leave(grad, back, mixed_t, up):
+
+
+def leave(grad, back, mixed_t, up, weight):
     unit = (8, 128)
     grad_shape = (grad.shape[1], grad.shape[0], grad.shape[2])
     back_shape = (back.shape[1], back.shape[0], back.shape[2])
@@ -346,13 +365,13 @@
     return pl.pallas_call(
         leave_kernel,
         out_shape=[
-            jax.ShapeDtypeStruct(grad_shape, BF),
-            jax.ShapeDtypeStruct(back_shape, BF),
+            jax.ShapeDtypeStruct((grad.shape[2], up.shape[0]), BF),
+            jax.ShapeDtypeStruct(up.shape, BF),
             jax.ShapeDtypeStruct((32, 3, 8, 128), BF),
         ],
-        in_specs=[pl.BlockSpec(memory_space=pltpu.VMEM)] * 4,
+        in_specs=[pl.BlockSpec(memory_space=pltpu.VMEM)] * 5,
         out_specs=[pl.BlockSpec(memory_space=pltpu.VMEM)] * 3,
-        scratch_shapes=[vm(grad_shape, BF), vm(back_shape, BF)] + [dma] * 6 + [
+        scratch_shapes=[vm(grad_shape, BF), vm(back_shape, BF)] * 2 + [dma] * 6 + [
             vm((4, 8, 4, 3) + unit, F32),
             vm((4 * HEAD_DIM, up.shape[0]), BF),
             vm(up.shape, BF),
@@ -372,9 +391,9 @@
             dma((7,)), dma((7,)),
             dma, dma,
         ],
-        compiler_params=pltpu.CompilerParams(collective_id=1, has_side_effects=True),
+        compiler_params=pltpu.CompilerParams(collective_id=1, has_side_effects=True, vmem_limit_bytes=16 * 2**20),
         name="leave",
-    )(grad, back, mixed_t, up)
+    )(grad, back, mixed_t, up, weight)
 
 
 def attend_all(stacked, grad_in, allowed, factor):
@@ -427,13 +446,10 @@
     mixed_t = mixed.reshape(frames * pos_here, HEADS // 2, 2, HEAD_DIM)
     mixed_t = mixed_t.transpose(2, 1, 3, 0).reshape(2, inner // 2, frames * pos_here)
     back = mixed.transpose(1, 0, 2, 3).reshape(pos_here, frames, inner)
-    qkv_grad, back, units = leave(packed_grad, back, mixed_t, up)
+    qkv_grad, output, units = leave(packed_grad, back, mixed_t, up, full_weight)
     units = units.reshape(96, 8, 128)[:81].reshape(9, 9, 8, 128)
     weight_grad = units.transpose(0, 2, 1, 3).reshape(HEAD_DIM, width).astype(F32)
-    output = jnp.dot(
-        back.reshape(positions, inner), full_weight, preferred_element_type=F32
-    ).astype(BF)
-    return (output.reshape(upstream.shape), qkv_grad.reshape(qkv.shape), weight_grad)
+    return (output.reshape(upstream.shape), qkv_grad.T.reshape(qkv.shape), weight_grad)
 
 
 def solution(mesh):

time: 106 us -> 100 us (0.943)
  local copies, waits for them, and re-layouts: 9.29 us -> 6.3 us
  Pallas kernels: 87.9 us -> 86.4 us
  matrix products: 4.72 us -> 3.53 us
    reshape x2 -> x0, local copies, waits for them, and re-layouts: 1.42 us -> none  [the longest x1 1.08 us: on_device(): back.reshape(positions, inner)]
    dot_general x1 -> x0, matrix products: 1.12 us -> none  [on_device(): jnp.dot(back.reshape(positions, inner), full_weight, preferred_element_ty...]
where the time goes in v5:
time: 100 us; the launch traced here: 99.8 us
  Pallas kernels  86.4 us (86%)
  local copies, waits for them, and re-layouts  6.3 us (6%)
  matrix products  3.53 us (4%)
  other arithmetic  2.74 us (3%)
    pallas_call x1, Pallas kernels, leave(): pl.pallas_call(leave_kernel, out_shape=[jax.ShapeDtypeStruct((grad.shape[...  44.3 us
    pallas_call x1, Pallas kernels, enter(): pl.pallas_call(enter_kernel, out_shape=[jax.ShapeDtypeStruct(qkv_shape, B...  42.1 us

profile of v5, /device:TPU:1, one launch (start us, length us, event | category | flops | bytes accessed | tf_op | source)
XLA Modules:
  0.0 99.8 jit_solution(4442508325320035079)
XLA Ops:
  0.6 42.1 %enter.1 = (bf16[64,2,1728]{2,1,0:T(2,128)(2,1)}, bf16[64,2,1152]{2,1,0:T(2,128)(2,1)}, bf16[8,9,8,1152]{3,2,1,0:T(8,128)(2,1)}) custom-call(bf16[1728,128]{1,0:T(8,128)(2,1)} %bitcast.73, bf16[128,1152]{1,0:T(8,128)(2,1)} %bitcast.74, bf16[9,8,1152]{2,1,0:T(8,128)(2,1)} %bitcast.75), custom_call_target="tpu_custom_call" | custom-call | tf_op jit(solution)/shard_map/enter/pallas_call | solution.py:195
  42.7 0.8 broadcast_compare_fusion
  43.5 1.1 %reshape.91.up_ref = bf16[128,1152]{1,0:T(8,128)(2,1)S(1)} reshape(bf16[64,2,1152]{2,1,0:T(2,128)(2,1)} %get-tuple-element.14) | data formatting | bytes 589824 | tf_op jit(solution)/shard_map/reshape | solution.py:440
  44.6 0.0 copy-start.1
  44.6 1.9 %convolution_convert_fusion.2 = bf16[128,576]{0,1:T(8,128)(2,1)S(1)} fusion(bf16[128,1152]{1,0:T(8,128)(2,1)S(1)} %reshape.91.up_ref, bf16[576,1152]{1,0:T(8,128)(2,1)} %bitcast.64), kind=kOutput, calls=%fused_computation.14 | convolution fusion | flops 169943040 | bytes 1769472 | tf_op jit(solution)/shard_map/dot_general | solution.py:442
  46.5 0.2 copy.18
  46.7 0.3 reshape.93
  47.0 0.0 copy-done.1
  47.0 1.4 %reshape.90 = bf16[64,2,3,8,72]{4,3,2,1,0:T(8,128)(2,1)S(1)} reshape(bf16[64,2,1728]{2,1,0:T(2,128)(2,1)S(1)} %copy-done.1) | data formatting | bytes 884736 | tf_op jit(solution)/shard_map/reshape | solution.py:401
  48.3 0.1 fusion.14
  48.5 0.3 fusion.3
  48.7 0.9 fusion.15
  49.6 0.3 convolution_convert_fusion
  50.0 0.3 fusion.8
  50.3 0.3 multiply_reduce_fusion
  50.5 0.1 multiply_convert_fusion
  50.7 0.2 fusion.6
  50.9 0.3 fusion.7
  51.2 0.2 maximum_bitcast_fusion
  51.4 0.5 copy.23
  51.9 0.0 copy-start
  51.9 0.5 reshape.94.grad_in
  52.4 0.2 copy.25
  52.6 0.2 reshape.95.back_in
  52.8 0.2 copy.26
  53.0 0.2 copy.27
  53.2 0.0 copy-done
  53.2 44.3 %leave.1 = (bf16[1728,128]{1,0:T(8,128)(2,1)S(1)}, bf16[128,1152]{1,0:T(8,128)(2,1)S(1)}, bf16[32,3,8,128]{3,2,1,0:T(8,128)(2,1)S(1)}) custom-call(bf16[2,64,1728]{2,1,0:T(8,128)(2,1)S(1)} %reshape.94.grad_in, bf16[2,64,576]{2,1,0:T(8,128)(2,1)S(1)} %reshape.95.back_in, bf16[2,288,128]{2,1,0:T(8,128)(2,1)S(1)} %bitcast.66, ...), custom_call_target="tpu_custom_call" | custom-call | tf_op jit(solution)/shard_map/leave/pallas_call | solution.py:365
  97.6 0.7 convert_bitcast_fusion
  98.3 0.7 copy.52
  99.0 0.8 copy.53
  (1 shorter events, 0.0 us)
Async XLA Ops:
  44.6 2.3 %copy-start.1 = (bf16[64,2,1728]{2,1,0:T(2,128)(2,1)S(1)}, bf16[64,2,1728]{2,1,0:T(2,128)(2,1)}, u32[]{:S(2)}) copy-start(bf16[64,2,1728]{2,1,0:T(2,128)(2,1)} %get-tuple-element.12) | copy-start | bytes 1327108
  51.9 1.3 %copy-start = (bf16[8,9,8,1152]{3,2,1,0:T(8,128)(2,1)S(1)}, bf16[8,9,8,1152]{3,2,1,0:T(8,128)(2,1)}, u32[]{:S(2)}) copy-start(bf16[8,9,8,1152]{3,2,1,0:T(8,128)(2,1)} %get-tuple-element.15) | copy-start | bytes 3981316
